TPU v7x, 512 devices: a whole 4x8x8 slice. The times are simulated.
512 devices in a mesh: fsdp: 8 (over z_hi, x), ctx: 16 (over y, core), tp: 4 (over z_lo).
Axes of the slice: x: 4, y: 8, z: 8 (z_hi: 2, z_lo: 4; z = z_hi * 4 + z_lo), core: 2. Of those that a mesh axis runs over, the one named last changes fastest.
Arguments:
- q_in: bfloat16 [8, 4096, 4096], P('fsdp', 'ctx', 'tp'), may hold values from -6 to 6
- k_in: bfloat16 [8, 4096, 4096], P('fsdp', 'ctx', 'tp'), may hold values from -6 to 6
- v_in: bfloat16 [8, 4096, 4096], P('fsdp', 'ctx', 'tp'), may hold values from -6 to 6
- grad_out: bfloat16 [8, 4096, 4096], P('fsdp', 'ctx', 'tp'), may hold values from -6 to 6
- genome_ids: int32 [8, 4096], P('fsdp', 'ctx'), may hold values from 0 to 31, never falling along the last dimension, each value on 1 to 1024 neighbouring positions
- long_filter: bfloat16 [256, 128], P('tp', 'fsdp'), may hold values from -0.5 to 0.5
- short_filter: float32 [3, 7, 4096], P(None, None, 'tp'), may hold values from -2 to 2
Outputs:
- grad_q: bfloat16 [8, 4096, 4096], P('fsdp', 'ctx', 'tp')
- grad_k: bfloat16 [8, 4096, 4096], P('fsdp', 'ctx', 'tp')
- grad_v: bfloat16 [8, 4096, 4096], P('fsdp', 'ctx', 'tp')
- grad_long: float32 [256, 128], P('tp', 'fsdp')
- grad_short: float32 [3, 7, 4096], P(None, None, 'tp')
Inputs may be any that keep to these rules, and one draw needn't show every extreme that they name: `genome_ids`: along each sequence the genome ids never fall; each genome covers 1 to 1024 positions, and one covers exactly that many.
All inputs are finite; a program needn't handle non-finite values.
Results may differ from a plain program's by a relative error of at most 0.005.
Values may be sent and summed in bfloat16 or wider, within the bound.
A program may use at most 128 MiB of HBM per device.

v0:
```python
import functools
import math

import jax
import jax.numpy as jnp
from jax import lax
from jax.experimental import pallas as pl
from jax.experimental.pallas import tpu as pltpu
from jax.sharding import PartitionSpec as P

TAPS = 128
SHORT = 7
LANES = 128
PAD = 8
TAIL = 16
F32 = jnp.float32
BF16 = jnp.bfloat16
MESH = pl.DeviceIdType.MESH

TAILS, IDS_DOWN, IDS_UP, U_HALO, DZ_HALO, HEADS, FIRST_FREE = 0, 3, 4, 5, 6, 7, 8


def kernel(
    dims,
    q_ref, k_ref, v_ref, g_ref, ids_ref, lf_ref, sf_ref,
    oq_ref, ok_ref, ov_ref, ogl_ref, ogs_ref,
    x32, ks_ref, vs_ref, u_ref, dz_ref, uh_ref, dzh_ref, tails_ref, idp_ref, idn_ref,
    lfs_ref, h_ref, hr_ref, bc_ref, ba_ref, mc_ref, ma_ref, maf_ref, idc_ref, ms_ref, mas_ref,
    d32, dh_ref, pay_ref, rs_ref, red_ref, fin_ref,
    ssem, rsem,
):
    C, F, remote = dims
    R = q_ref.shape[1]
    T = q_ref.shape[2] // LANES
    B = R // TAPS
    G, tapw = lf_ref.shape
    GT = G // T
    width = LANES // GT
    NT = pay_ref.shape[0]
    per = NT // C
    ctx = lax.axis_index("ctx") if remote else 0
    fs = lax.axis_index("fsdp") if remote else 0
    nxt = {"ctx": lax.rem(ctx + 1, C)}
    prv = {"ctx": lax.rem(ctx + C - 1, C)}
    fil0 = FIRST_FREE
    rs0 = fil0 + F
    red0 = rs0 + C
    ag0 = red0 + F

    def rcopy(src, dst, slot, device):
        return pltpu.make_async_remote_copy(
            src_ref=src, dst_ref=dst, send_sem=ssem.at[slot], recv_sem=rsem.at[slot],
            device_id=device, device_id_type=MESH,
        )

    def ctx_peer(d):
        return lax.rem(ctx + d, C)

    def fs_peer(d):
        return lax.rem(fs + d, F)

    if remote:
        barrier = pltpu.get_barrier_semaphore()
        for d in range(1, C):
            pl.semaphore_signal(barrier, inc=1, device_id={"ctx": ctx_peer(d)}, device_id_type=MESH)
        for d in range(1, F):
            pl.semaphore_signal(barrier, inc=1, device_id={"fsdp": fs_peer(d)}, device_id_type=MESH)

    def fill_columns(row, chunk):
        idc_ref[chunk * LANES:(chunk + 1) * LANES, :] = jnp.transpose(
            jnp.broadcast_to(row, (LANES, LANES))
        )

    own_ids = ids_ref[...].astype(F32)
    for b in range(B):
        fill_columns(own_ids[:, b * LANES:(b + 1) * LANES], 1 + b)

    def fill_short_masks(r0, n):
        here = idc_ref[pl.ds(LANES + r0, n), :]
        for j in range(1, SHORT):
            back = idc_ref[pl.ds(LANES + r0 - j, n), :]
            ms_ref[j - 1, pl.ds(r0, n), :] = jnp.where(here == back, 1.0, 0.0)

    fill_short_masks(TAIL, R - TAIL)

    def lane_block(t):
        return pl.ds(pl.multiple_of(t * LANES, LANES), LANES)

    def widen(t, carry):
        for i, ref in enumerate((q_ref, k_ref, v_ref)):
            x32[i, t, PAD:PAD + R, :] = ref[0, :, lane_block(t)].astype(F32)
        return carry

    lax.fori_loop(0, T, widen, 0)

    if remote:
        pl.semaphore_wait(barrier, (C - 1) + (F - 1))
        tail_copies = [
            rcopy(ref.at[0, pl.ds(R - TAIL, TAIL), :], tails_ref.at[i], TAILS + i, nxt)
            for i, ref in enumerate((q_ref, k_ref, v_ref))
        ]
        ids_down = rcopy(ids_ref, idp_ref, IDS_DOWN, nxt)
        ids_up = rcopy(ids_ref, idn_ref, IDS_UP, prv)
        for copy in tail_copies + [ids_down, ids_up]:
            copy.start()
        filter_sends = [
            rcopy(lf_ref, lfs_ref.at[fs], fil0 + d, {"fsdp": fs_peer(d)}) for d in range(1, F)
        ]
        for copy in filter_sends:
            copy.start()
    lfs_ref[fs] = lf_ref[...]

    def short_rows(t, r0, n):
        convs = []
        for i in range(3):
            total = x32[i, t, pl.ds(PAD + r0, n), :] * sf_ref[i, 0:1, lane_block(t)]
            for j in range(1, SHORT):
                piece = x32[i, t, pl.ds(PAD + r0 - j, n), :] * ms_ref[j - 1, pl.ds(r0, n), :]
                total = total + piece * sf_ref[i, j:j + 1, lane_block(t)]
            convs.append(total)
        qs, ks, vs = convs
        ks_ref[t, pl.ds(r0, n), :] = ks
        vs_ref[t, pl.ds(r0, n), :] = vs
        u_ref[t, pl.ds(r0, n), :] = (ks * vs).astype(BF16)
        upstream = g_ref[0, pl.ds(r0, n), lane_block(t)].astype(F32)
        dz_ref[t, pl.ds(r0, n), :] = (upstream * qs).astype(BF16)

    def short_main(t, carry):
        short_rows(t, TAIL, R - TAIL)
        return carry

    lax.fori_loop(0, T, short_main, 0)

    if remote:
        u_copy = rcopy(u_ref.at[:, pl.ds(R - TAPS, TAPS), :], uh_ref, U_HALO, nxt)
        u_copy.start()
        for copy in tail_copies + [ids_down, ids_up]:
            copy.wait()

    prev_ids = idp_ref[...].astype(F32)[:, R - LANES:]
    next_ids = idn_ref[...].astype(F32)[:, :LANES]
    if remote:
        prev_ids = jnp.where(ctx == 0, -1.0, prev_ids)
        next_ids = jnp.where(ctx == C - 1, -1.0, next_ids)
    fill_columns(prev_ids, 0)
    fill_columns(next_ids, 1 + B)
    fill_short_masks(0, TAIL)

    def short_head(t, carry):
        for i in range(3):
            x32[i, t, 0:PAD, :] = tails_ref[i, :, lane_block(t)].astype(F32)[TAIL - PAD:]
        short_rows(t, 0, TAIL)
        return carry

    lax.fori_loop(0, T, short_head, 0)

    if remote:
        dz_copy = rcopy(dz_ref.at[:, pl.ds(0, TAPS), :], dzh_ref, DZ_HALO, prv)
        dz_copy.start()

    for j in range(1, SHORT):
        ahead = idc_ref[pl.ds(LANES + j, R), :]
        mas_ref[j - 1] = jnp.where(idc_ref[pl.ds(LANES, R), :] == ahead, 1.0, 0.0)
    rows = [prev_ids] + [own_ids[:, b * LANES:(b + 1) * LANES] for b in range(B)] + [next_ids]
    for b in range(B):
        column = idc_ref[(1 + b) * LANES:(2 + b) * LANES, :]
        for half in range(2):
            back = jnp.where(column == rows[b + half], 1.0, 0.0)
            ahead = jnp.where(column == rows[b + 1 + half], 1.0, 0.0)
            mc_ref[b, :, half * LANES:(half + 1) * LANES] = back.astype(BF16)
            ma_ref[b, :, half * LANES:(half + 1) * LANES] = ahead.astype(BF16)
            maf_ref[b, :, half * LANES:(half + 1) * LANES] = ahead

    if remote:
        for d in range(1, F):
            rcopy(lf_ref, lfs_ref.at[lax.rem(fs + F - d, F)], fil0 + d, {"fsdp": fs_peer(d)}).wait_recv()
    taps = jnp.zeros((G, TAPS), F32)
    flipped = jnp.zeros((G, TAPS), F32)
    place_row = lax.broadcasted_iota(jnp.int32, (tapw, TAPS), 0)
    place_col = lax.broadcasted_iota(jnp.int32, (tapw, TAPS), 1)
    for s in range(F):
        own = jnp.where(place_col == place_row + s * tapw, 1.0, 0.0).astype(BF16)
        turned = jnp.where(place_col == TAPS - 1 - s * tapw - place_row, 1.0, 0.0).astype(BF16)
        taps = taps + jnp.dot(lfs_ref[s], own, preferred_element_type=F32)
        flipped = flipped + jnp.dot(lfs_ref[s], turned, preferred_element_type=F32)
    h_ref[:, :TAPS] = taps
    h_ref[:, TAPS:] = jnp.zeros((G, TAPS), F32)
    hr_ref[:, :TAPS] = flipped
    hr_ref[:, TAPS:] = jnp.zeros((G, TAPS), F32)
    sub = lax.broadcasted_iota(jnp.int32, (8, 2 * TAPS), 0)

    def band_of(base, extra):
        for bit in (1, 2, 4):
            base = jnp.where((sub & bit) != 0, pltpu.roll(base, bit, 1), base)
        if extra:
            base = pltpu.roll(base, extra, 1)
        parts = [base] + [pltpu.roll(base, 8 * a, 1) for a in range(1, TAPS // 8)]
        return jnp.concatenate(parts, axis=0).astype(BF16)

    def build(g, carry):
        ba_ref[g] = band_of(jnp.broadcast_to(h_ref[pl.ds(g, 1), :], (8, 2 * TAPS)), 0)
        bc_ref[g] = band_of(jnp.broadcast_to(hr_ref[pl.ds(g, 1), :], (8, 2 * TAPS)), 1)
        return carry

    lax.fori_loop(0, G, build, 0)

    if remote:
        u_copy.wait()
        dz_copy.wait()
    lane_group = lax.broadcasted_iota(jnp.int32, (TAPS, LANES), 1) // width

    def dz_window(t, b):
        if b + 1 < B:
            return dz_ref[t, b * TAPS:(b + 2) * TAPS, :]
        return jnp.concatenate([dz_ref[t, b * TAPS:, :], dzh_ref[t]], axis=0)

    def u_window(t, b):
        if b > 0:
            return u_ref[t, (b - 1) * TAPS:(b + 1) * TAPS, :]
        return jnp.concatenate([uh_ref[t], u_ref[t, :TAPS, :]], axis=0)

    def banded(band_ref, mask, t, window):
        weights = band_ref[pl.ds(t * GT, GT)] * mask[None]
        product = jnp.dot(
            weights.reshape(GT * TAPS, 2 * TAPS), window, preferred_element_type=F32
        ).reshape(GT, TAPS, LANES)
        total = product[0]
        for g in range(1, GT):
            total = jnp.where(lane_group == g, product[g], total)
        return total

    def long_products(t, carry):
        for b in range(B):
            here = pl.ds(b * TAPS, TAPS)
            du = banded(ba_ref, ma_ref[b], t, dz_window(t, b))
            d32[1, t, here, :] = du * vs_ref[t, here, :]
            d32[2, t, here, :] = du * ks_ref[t, here, :]
            z = banded(bc_ref, mc_ref[b], t, u_window(t, b))
            d32[0, t, here, :] = g_ref[0, here, lane_block(t)].astype(F32) * z
        return carry

    lax.fori_loop(0, T, long_products, 0)
    if remote:
        heads = rcopy(d32.at[:, :, pl.ds(0, PAD), :], dh_ref, HEADS, prv)
        heads.start()

    long_scale = 1.0 / math.sqrt(dims_count(C, F, R) * width)
    short_scale = 1.0 / math.sqrt(dims_count(C, F, R))
    lane_row = lax.broadcasted_iota(jnp.int32, (1, LANES), 1) // width
    group_lanes = [jnp.where(lane_row == g, 1.0, 0.0).astype(BF16) for g in range(GT)]
    sub_all = lax.broadcasted_iota(jnp.int32, (GT * 8, 2 * TAPS), 0) & 7

    def long_grad(t, carry):
        sums = [None] * GT
        for b in range(B):
            signal = u_ref[t, b * TAPS:(b + 1) * TAPS, :]
            left = jnp.concatenate([signal * group_lanes[g] for g in range(GT)], axis=0)
            product = lax.dot_general(
                left, dz_window(t, b), (((1,), (1,)), ((), ())), preferred_element_type=F32
            )
            mask = maf_ref[b]
            for g in range(GT):
                part = product[g * TAPS:(g + 1) * TAPS] * mask
                sums[g] = part if sums[g] is None else sums[g] + part
        folded = []
        for g in range(GT):
            total = sums[g][0:8]
            for a in range(1, TAPS // 8):
                total = total + pltpu.roll(sums[g][8 * a:8 * a + 8], 2 * TAPS - 8 * a, 1)
            folded.append(total)
        stack = jnp.concatenate(folded, axis=0)
        for bit in (1, 2, 4):
            stack = jnp.where((sub_all & bit) != 0, pltpu.roll(stack, 2 * TAPS - bit, 1), stack)
        lags = jnp.sum(stack[:, :TAPS].reshape(GT, 8, TAPS), axis=1)
        pay_ref[3 * T + t] = lags * long_scale
        return carry

    lax.fori_loop(0, T, long_grad, 0)

    if remote:
        heads.wait()
    d32[:, :, R:R + PAD, :] = dh_ref[...]

    def short_grads(t, carry):
        for i in range(3):
            source = x32[i, t, PAD:PAD + R, :]
            sums = []
            for j in range(SHORT):
                term = d32[i, t, pl.ds(j, R), :] * source
                if j:
                    term = term * mas_ref[j - 1]
                sums.append(jnp.sum(term, axis=0, keepdims=True))
            sums.append(jnp.zeros((1, LANES), F32))
            pay_ref[i * T + t] = jnp.concatenate(sums, axis=0) * short_scale
        return carry

    lax.fori_loop(0, T, short_grads, 0)

    def own_slots(owner):
        return pl.ds(owner * per, per)

    if remote:
        scatter = [
            rcopy(pay_ref.at[own_slots(ctx_peer(d))], rs_ref.at[ctx], rs0 + d, {"ctx": ctx_peer(d)})
            for d in range(1, C)
        ]
        for copy in scatter:
            copy.start()
        rs_ref[ctx] = pay_ref[own_slots(ctx)]

    def outputs(i, o_ref):
        def one(t, carry):
            total = d32[i, t, pl.ds(0, R), :] * sf_ref[i, 0:1, lane_block(t)]
            for j in range(1, SHORT):
                piece = d32[i, t, pl.ds(j, R), :] * mas_ref[j - 1]
                total = total + piece * sf_ref[i, j:j + 1, lane_block(t)]
            o_ref[0, :, lane_block(t)] = total.astype(BF16)
            return carry

        lax.fori_loop(0, T, one, 0)

    outputs(0, oq_ref)
    if remote:
        for d in range(1, C):
            sender = lax.rem(ctx + C - d, C)
            rcopy(pay_ref.at[own_slots(ctx)], rs_ref.at[sender], rs0 + d, {"ctx": ctx_peer(d)}).wait_recv()
        total = rs_ref[0]
        for c in range(1, C):
            total = total + rs_ref[c]
        red_ref[fs] = total
        exchange = [
            rcopy(red_ref.at[fs], red_ref.at[fs], red0 + d, {"fsdp": fs_peer(d)}) for d in range(1, F)
        ]
        for copy in exchange:
            copy.start()
    outputs(1, ok_ref)
    if remote:
        for d in range(1, F):
            sender = lax.rem(fs + F - d, F)
            rcopy(red_ref.at[fs], red_ref.at[sender], red0 + d, {"fsdp": fs_peer(d)}).wait_recv()
        total = red_ref[0]
        for f in range(1, F):
            total = total + red_ref[f]
        fin_ref[own_slots(ctx)] = total
        gather = [
            rcopy(fin_ref.at[own_slots(ctx)], fin_ref.at[own_slots(ctx)], ag0 + d, {"ctx": ctx_peer(d)})
            for d in range(1, C)
        ]
        for copy in gather:
            copy.start()
    outputs(2, ov_ref)
    if remote:
        for d in range(1, C):
            sender = lax.rem(ctx + C - d, C)
            rcopy(
                fin_ref.at[own_slots(ctx)], fin_ref.at[own_slots(sender)], ag0 + d, {"ctx": ctx_peer(d)}
            ).wait_recv()
    for i in range(3):
        for t in range(T):
            ogs_ref[i, :, t * LANES:(t + 1) * LANES] = fin_ref[i * T + t, 0:SHORT, :]
    lags = fin_ref[3 * T:4 * T].reshape(G, TAPS)
    shift = lax.rem(TAPS - fs * tapw, TAPS)
    ogl_ref[...] = pltpu.roll(lags, shift, 1)[:, :tapw]
    if remote:
        for copy in filter_sends + scatter + exchange + gather:
            copy.wait_send()


def dims_count(contexts, sequences, rows):
    return contexts * sequences * rows


def mixer(C, F, remote, q_in, k_in, v_in, grad_out, ids, long_filter, short_filter):
    R, channels = q_in.shape[1], q_in.shape[2]
    T, B = channels // LANES, R // TAPS
    G, tapw = long_filter.shape
    NT = 4 * T
    per = NT // C
    wide = jax.ShapeDtypeStruct(q_in.shape, BF16)
    copies = FIRST_FREE + 2 * F + 2 * C
    vmem = pltpu.VMEM
    return pl.pallas_call(
        functools.partial(kernel, (C, F, remote)),
        out_shape=(
            wide, wide, wide,
            jax.ShapeDtypeStruct((G, tapw), F32),
            jax.ShapeDtypeStruct(short_filter.shape, F32),
        ),
        in_specs=[pl.BlockSpec(memory_space=vmem)] * 7,
        out_specs=[pl.BlockSpec(memory_space=vmem)] * 5,
        scratch_shapes=[
            vmem((3, T, PAD + R, LANES), F32),
            vmem((T, R, LANES), F32), vmem((T, R, LANES), F32),
            vmem((T, R, LANES), BF16), vmem((T, R, LANES), BF16),
            vmem((T, TAPS, LANES), BF16), vmem((T, TAPS, LANES), BF16),
            vmem((3, TAIL, channels), BF16),
            vmem((1, R), jnp.int32), vmem((1, R), jnp.int32),
            vmem((F, G, tapw), BF16),
            vmem((G, 2 * TAPS), F32), vmem((G, 2 * TAPS), F32),
            vmem((G, TAPS, 2 * TAPS), BF16), vmem((G, TAPS, 2 * TAPS), BF16),
            vmem((B, TAPS, 2 * TAPS), BF16), vmem((B, TAPS, 2 * TAPS), BF16),
            vmem((B, TAPS, 2 * TAPS), F32),
            vmem((R + 2 * LANES, LANES), F32),
            vmem((SHORT - 1, R, LANES), F32), vmem((SHORT - 1, R, LANES), F32),
            vmem((3, T, R + PAD, LANES), F32),
            vmem((3, T, PAD, LANES), F32),
            vmem((NT, 8, LANES), F32),
            vmem((C, per, 8, LANES), F32),
            vmem((F, per, 8, LANES), F32),
            vmem((NT, 8, LANES), F32),
            pltpu.SemaphoreType.DMA((copies,)),
            pltpu.SemaphoreType.DMA((copies,)),
        ],
        compiler_params=pltpu.CompilerParams(
            collective_id=0 if remote else None,
            has_side_effects=True,
            vmem_limit_bytes=60 * 1024 * 1024,
        ),
        name="mixer",
    )(q_in, k_in, v_in, grad_out, ids, long_filter, short_filter)


def solution(mesh):
    C, F = mesh.shape["ctx"], mesh.shape["fsdp"]
    wide = P("fsdp", "ctx", "tp")
    return jax.shard_map(
        functools.partial(mixer, C, F, True),
        mesh=mesh,
        in_specs=(wide, wide, wide, wide, P("fsdp", "ctx"), P("tp", "fsdp"), P(None, None, "tp")),
        out_specs=(wide, wide, wide, P("tp", "fsdp"), P(None, None, "tp")),
        check_vma=False,
    )
```

profile of v0, /device:TPU:1, one launch (start us, length us, event | category | flops | bytes accessed | tf_op | source)
XLA Modules:
  0.0 88.6 jit_solution(16105523688395030913)
XLA Ops:
  0.6 1.4 %copy.12.lf_ref = bf16[64,16]{1,0:T(8,128)(2,1)} copy(bf16[64,16]{0,1:T(8,128)(2,1)} %param.12) | data formatting | bytes 4096 | tf_op args[5]
  2.0 80.3 %mixer.1 = (bf16[1,256,1024]{2,1,0:T(8,128)(2,1)}, bf16[1,256,1024]{2,1,0:T(8,128)(2,1)}, bf16[1,256,1024]{2,1,0:T(8,128)(2,1)}, f32[64,16]{1,0:T(8,128)}, f32[3,7,1024]{2,1,0:T(8,128)}) custom-call(bf16[1,256,1024]{2,1,0:T(8,128)(2,1)} %q_ref.1, bf16[1,256,1024]{2,1,0:T(8,128)(2,1)} %k_ref.1, bf16[1,256,1024]{2,1,0:T(8,128)(2,1)} %v_ref.1, ...), custom_call_target="tpu_custom_call" | custom-call | tf_op jit(solution)/shard_map/mixer/pallas_call | solution.py:382
  82.4 1.4 %copy.13 = f32[64,16]{0,1:T(8,128)} copy(f32[64,16]{1,0:T(8,128)} %get-tuple-element.8) | data formatting | bytes 8192 | tf_op jit(solution)/shard_map/mixer/pallas_call | solution.py:382
  83.8 0.0 copy-start.1
  83.8 1.9 %copy.18 = bf16[1,256,1024]{2,1,0:T(8,128)(2,1)} copy(bf16[1,256,1024]{2,1,0:T(8,128)(2,1)} %get-tuple-element.15) | data formatting | bytes 1048576
  85.7 0.0 copy-done.1
  85.7 0.0 copy-start
  85.7 0.8 copy.19
  86.5 0.4 copy-done
  86.9 0.0 copy-start.2
  86.9 0.8 copy.20
  87.7 0.2 copy-done.2
  87.9 0.6 copy.21
Async XLA Ops:
  83.8 1.9 %copy-start.1 = (bf16[1,256,1024]{2,1,0:T(8,128)(2,1)S(1)}, bf16[1,256,1024]{2,1,0:T(8,128)(2,1)}, u32[]{:S(2)}) copy-start(bf16[1,256,1024]{2,1,0:T(8,128)(2,1)} %get-tuple-element.16) | copy-start | bytes 1572868
  85.7 1.2 %copy-start = (bf16[1,256,1024]{2,1,0:T(8,128)(2,1)S(1)}, bf16[1,256,1024]{2,1,0:T(8,128)(2,1)}, u32[]{:S(2)}) copy-start(bf16[1,256,1024]{2,1,0:T(8,128)(2,1)} %get-tuple-element.17) | copy-start | bytes 1572868
  86.9 1.0 %copy-start.2 = (f32[3,7,1024]{2,1,0:T(8,128)S(1)}, f32[3,7,1024]{2,1,0:T(8,128)}, u32[]{:S(2)}) copy-start(f32[3,7,1024]{2,1,0:T(8,128)} %get-tuple-element.19) | copy-start | bytes 258052
where the time goes:
time: 88.9 us; the launch traced here: 88.6 us
  Pallas kernels  80.3 us (90%)
  local copies, waits for them, and re-layouts  7.57 us (9%)
    pallas_call x1, Pallas kernels, mixer(): pl.pallas_call(functools.partial(kernel, (C, F, remote)), out_shape=(wide...  80.3 us
    unnamed x11, local copies, waits for them, and re-layouts  6.14 us

commit v1 on v0

v1 whole, which is shorter than its diff:
```python
import functools
import math

import jax
import jax.numpy as jnp
from jax import lax
from jax.experimental import pallas as pl
from jax.experimental.pallas import tpu as pltpu
from jax.sharding import PartitionSpec as P

TAPS = 128
SHORT = 7
LANES = 128
PAD = 8
TAIL = 16
CHUNK = 64
F32 = jnp.float32
BF16 = jnp.bfloat16
MESH = pl.DeviceIdType.MESH
NT_DIMS = (((1,), (1,)), ((), ()))

TAILS, IDS_DOWN, IDS_UP, U_HALO, DZ_HALO, HEADS, FIRST_FREE = 0, 3, 4, 5, 6, 7, 10


def kernel(
    dims,
    q_hbm, k_hbm, v_hbm, g_hbm, ids_hbm, lf_hbm, sf_hbm,
    oq_hbm, ok_hbm, ov_hbm, ogl_ref, ogs_ref,
    xin_ref, g_ref, ids_ref, lf_ref, sf_ref, out_ref,
    x32, pm_ref, ks_ref, vs_ref, u_ref, dz_ref, uh_ref, dzh_ref, ut_ref, dzt_ref,
    tails_ref, idp_ref, idn_ref,
    lfs_ref, h_ref, hn_ref, ba_ref, bc_ref, mc_ref, ma_ref, mq_ref, idc_ref, ms_ref, mas_ref,
    d32, dh_ref, gl_ref, turn_ref, pay_ref, rs_ref, red_ref, fin_ref,
    ssem, rsem, isem, osem,
):
    C, F, remote = dims
    R = xin_ref.shape[1]
    T = xin_ref.shape[2] // LANES
    B = R // TAPS
    tapw, G = lf_ref.shape
    GT = G // T
    width = LANES // GT
    per = 2 * T // C
    ctx = lax.axis_index("ctx") if remote else 0
    fs = lax.axis_index("fsdp") if remote else 0
    nxt = {"ctx": lax.rem(ctx + 1, C)}
    prv = {"ctx": lax.rem(ctx + C - 1, C)}
    fil0 = FIRST_FREE
    rs0 = fil0 + F
    red0 = rs0 + 2 * C
    ag0 = red0 + 2 * F

    def rcopy(src, dst, slot, device):
        return pltpu.make_async_remote_copy(
            src_ref=src, dst_ref=dst, send_sem=ssem.at[slot], recv_sem=rsem.at[slot],
            device_id=device, device_id_type=MESH,
        )

    def ctx_peer(d):
        return lax.rem(ctx + d, C)

    def fs_peer(d):
        return lax.rem(fs + d, F)

    if remote:
        barrier = pltpu.get_barrier_semaphore()
        for d in range(1, C):
            pl.semaphore_signal(barrier, inc=1, device_id={"ctx": ctx_peer(d)}, device_id_type=MESH)
        for d in range(1, F):
            pl.semaphore_signal(barrier, inc=1, device_id={"fsdp": fs_peer(d)}, device_id_type=MESH)

    loads = [
        pltpu.make_async_copy(src, dst, isem.at[n])
        for n, (src, dst) in enumerate((
            (ids_hbm, ids_ref), (q_hbm.at[0], xin_ref.at[0]), (k_hbm.at[0], xin_ref.at[1]),
            (v_hbm.at[0], xin_ref.at[2]), (sf_hbm, sf_ref), (g_hbm.at[0], g_ref), (lf_hbm, lf_ref),
        ))
    ]
    for load in loads:
        load.start()
    loads[0].wait()

    def fill_columns(row, chunk):
        idc_ref[chunk * LANES:(chunk + 1) * LANES, :] = jnp.transpose(
            jnp.broadcast_to(row, (LANES, LANES))
        )

    own_ids = ids_ref[...].astype(F32)
    for b in range(B):
        fill_columns(own_ids[:, b * LANES:(b + 1) * LANES], 1 + b)

    def fill_short_masks(r0, n):
        here = idc_ref[pl.ds(LANES + r0, n), :]
        for j in range(1, SHORT):
            back = idc_ref[pl.ds(LANES + r0 - j, n), :]
            ms_ref[j - 1, pl.ds(r0, n), :] = jnp.where(here == back, 1.0, 0.0)

    fill_short_masks(TAIL, R - TAIL)

    def lane_block(t):
        return pl.ds(pl.multiple_of(t * LANES, LANES), LANES)

    for load in loads[1:6]:
        load.wait()

    def widen(t, carry):
        for i in range(3):
            x32[i, t, PAD:PAD + R, :] = xin_ref[i, :, lane_block(t)].astype(F32)
        return carry

    def short_rows(t, r0, n):
        convs = []
        for i in range(3):
            total = x32[i, t, pl.ds(PAD + r0, n), :] * sf_ref[i, 0:1, lane_block(t)]
            for j in range(1, SHORT):
                piece = x32[i, t, pl.ds(PAD + r0 - j, n), :] * ms_ref[j - 1, pl.ds(r0, n), :]
                pm_ref[i, j - 1, t, pl.ds(r0, n), :] = piece
                total = total + piece * sf_ref[i, j:j + 1, lane_block(t)]
            convs.append(total)
        qs, ks, vs = convs
        ks_ref[t, pl.ds(r0, n), :] = ks
        vs_ref[t, pl.ds(r0, n), :] = vs
        u_ref[t, pl.ds(r0, n), :] = (ks * vs).astype(BF16)
        upstream = g_ref[pl.ds(r0, n), lane_block(t)].astype(F32)
        dz_ref[t, pl.ds(r0, n), :] = (upstream * qs).astype(BF16)

    def short_main(t, carry):
        widen(t, carry)
        short_rows(t, TAIL, CHUNK - TAIL)
        for r0 in range(CHUNK, R, CHUNK):
            short_rows(t, r0, CHUNK)
        return carry

    early = (T + 1) // 2
    lax.fori_loop(0, early, short_main, 0)

    loads[6].wait()
    if remote:
        pl.semaphore_wait(barrier, (C - 1) + (F - 1))
        filter_sends = [
            rcopy(lf_ref, lfs_ref.at[fs], fil0 + d, {"fsdp": fs_peer(d)}) for d in range(1, F)
        ]
        tail_copies = [
            rcopy(xin_ref.at[i, pl.ds(R - TAIL, TAIL), :], tails_ref.at[i], TAILS + i, nxt)
            for i in range(3)
        ]
        ids_down = rcopy(ids_ref, idp_ref, IDS_DOWN, nxt)
        ids_up = rcopy(ids_ref, idn_ref, IDS_UP, prv)
        for copy in filter_sends + [ids_down, ids_up] + tail_copies:
            copy.start()
    lfs_ref[fs] = lf_ref[...]
    lax.fori_loop(early, T, short_main, 0)

    if remote:
        u_copy = rcopy(u_ref.at[:, pl.ds(R - TAPS, TAPS), :], uh_ref, U_HALO, nxt)
        u_copy.start()
        for copy in tail_copies + [ids_down, ids_up]:
            copy.wait()

    prev_ids = idp_ref[...].astype(F32)[:, R - LANES:]
    next_ids = idn_ref[...].astype(F32)[:, :LANES]
    if remote:
        prev_ids = jnp.where(ctx == 0, -1.0, prev_ids)
        next_ids = jnp.where(ctx == C - 1, -1.0, next_ids)
    fill_columns(prev_ids, 0)
    fill_columns(next_ids, 1 + B)
    fill_short_masks(0, TAIL)

    def short_head(t, carry):
        for i in range(3):
            x32[i, t, 0:PAD, :] = tails_ref[i, :, lane_block(t)].astype(F32)[TAIL - PAD:]
        short_rows(t, 0, TAIL)
        return carry

    lax.fori_loop(0, T, short_head, 0)

    if remote:
        dz_copy = rcopy(dz_ref.at[:, pl.ds(0, TAPS), :], dzh_ref, DZ_HALO, prv)
        dz_copy.start()

    for j in range(1, SHORT):
        ahead = idc_ref[pl.ds(LANES + j, R), :]
        mas_ref[j - 1] = jnp.where(idc_ref[pl.ds(LANES, R), :] == ahead, 1.0, 0.0)
    rows = [prev_ids] + [own_ids[:, b * LANES:(b + 1) * LANES] for b in range(B)] + [next_ids]
    row_index = lax.broadcasted_iota(jnp.int32, (TAPS, LANES), 0)
    col_index = lax.broadcasted_iota(jnp.int32, (TAPS, LANES), 1)
    one = jnp.ones((TAPS, LANES), F32)
    zero = jnp.zeros((TAPS, LANES), F32)
    upper = jnp.where(col_index >= row_index, one, zero)
    above = jnp.where(col_index > row_index, one, zero)
    for b in range(B):
        column = idc_ref[(1 + b) * LANES:(2 + b) * LANES, :]
        same = [jnp.where(column == rows[b + n], one, zero) for n in range(3)]
        mc_ref[b, 0] = (same[0] * above).astype(BF16)
        mc_ref[b, 1] = (same[1] * (one - above)).astype(BF16)
        ma_ref[b, 0] = (same[1] * upper).astype(BF16)
        ma_ref[b, 1] = (same[2] * (one - upper)).astype(BF16)
        mq_ref[b] = same[1] * upper + same[2] * (one - upper)

    def dz_window(t, b):
        if b + 1 < B:
            return dz_ref[t, b * TAPS:(b + 2) * TAPS, :]
        return jnp.concatenate([dz_ref[t, b * TAPS:, :], dzh_ref[t]], axis=0)

    lane_row = lax.broadcasted_iota(jnp.int32, (1, LANES), 1) // width
    group_lanes = [jnp.where(lane_row == g, 1.0, 0.0).astype(BF16) for g in range(GT)]
    in_upper = col_index >= row_index

    def long_grad(t, b):
        signal = u_ref[t, b * TAPS:(b + 1) * TAPS, :]
        left = jnp.concatenate([signal * group_lanes[g] for g in range(GT)], axis=0)
        product = lax.dot_general(left, dz_window(t, b), NT_DIMS, preferred_element_type=F32)
        mask = mq_ref[b]
        folded = []
        for g in range(GT):
            part = product[g * TAPS:(g + 1) * TAPS]
            part = jnp.where(in_upper, part[:, :LANES], part[:, LANES:]) * mask
            total = part[0:8]
            for a in range(1, TAPS // 8):
                total = total + pltpu.roll(part[8 * a:8 * a + 8], LANES - 8 * a, 1)
            folded.append(total)
        return jnp.concatenate(folded, axis=0)

    def early_grad(t, carry):
        total = long_grad(t, 0)
        for b in range(1, B - 1):
            total = total + long_grad(t, b)
        gl_ref[t] = total
        return carry

    lax.fori_loop(0, T, early_grad, 0, unroll=2)

    def turn_own(t, carry):
        for b in range(B):
            ut_ref[t, 1 + b] = jnp.transpose(u_ref[t, b * TAPS:(b + 1) * TAPS, :])
            dzt_ref[t, b] = jnp.transpose(dz_ref[t, b * TAPS:(b + 1) * TAPS, :])
        return carry

    lax.fori_loop(0, T, turn_own, 0)

    if remote:
        for d in range(1, F):
            rcopy(lf_ref, lfs_ref.at[lax.rem(fs + F - d, F)], fil0 + d, {"fsdp": fs_peer(d)}).wait_recv()
    stacked = jnp.concatenate([lfs_ref[s] for s in range(F)], axis=0)
    unit_row = lax.broadcasted_iota(jnp.int32, (G, G), 0)
    unit_col = lax.broadcasted_iota(jnp.int32, (G, G), 1)
    unit = jnp.where(unit_row == unit_col, 1.0, 0.0).astype(BF16)
    taps = lax.dot_general(unit, stacked, NT_DIMS, preferred_element_type=F32)
    swap = jnp.where(((row_index + col_index) & (TAPS - 1)) == 0, 1.0, 0.0).astype(BF16)
    h_ref[...] = taps
    hn_ref[...] = jnp.dot(taps.astype(BF16), swap, preferred_element_type=F32)
    sub = lax.broadcasted_iota(jnp.int32, (8, TAPS), 0)
    unroll = 4

    def band_of(row):
        base = jnp.broadcast_to(row, (8, TAPS))
        for bit in (1, 2, 4):
            base = jnp.where((sub & bit) != 0, pltpu.roll(base, bit, 1), base)
        parts = [base] + [pltpu.roll(base, 8 * a, 1) for a in range(1, TAPS // 8)]
        return jnp.concatenate(parts, axis=0).astype(BF16)

    def build(n, carry):
        for m in range(unroll):
            g = n * unroll + m
            ba_ref[g] = band_of(h_ref[pl.ds(g, 1), :])
            bc_ref[g] = band_of(hn_ref[pl.ds(g, 1), :])
        return carry

    lax.fori_loop(0, G // unroll, build, 0)

    def banded(band_ref, mask_ref, b, t, left_ref, first):
        parts = []
        for g in range(GT):
            band = band_ref[t * GT + g]
            weights = jnp.concatenate([band * mask_ref[b, 0], band * mask_ref[b, 1]], axis=1)
            rows_g = slice(g * width, (g + 1) * width)
            left = jnp.concatenate([left_ref[t, first, rows_g, :], left_ref[t, first + 1, rows_g, :]], axis=1)
            parts.append(lax.dot_general(left, weights, NT_DIMS, preferred_element_type=F32))
        return jnp.transpose(jnp.concatenate(parts, axis=0))

    def backward_rows(t, b):
        here = pl.ds(b * TAPS, TAPS)
        du = banded(ba_ref, ma_ref, b, t, dzt_ref, b)
        d32[1, t, here, :] = du * vs_ref[t, here, :]
        d32[2, t, here, :] = du * ks_ref[t, here, :]

    def forward_rows(t, b):
        here = pl.ds(b * TAPS, TAPS)
        z = banded(bc_ref, mc_ref, b, t, ut_ref, b)
        d32[0, t, here, :] = g_ref[here, lane_block(t)].astype(F32) * z

    def inner_products(t, carry):
        for b in range(B - 1):
            backward_rows(t, b)
        for b in range(1, B):
            forward_rows(t, b)
        return carry

    lax.fori_loop(0, T, inner_products, 0, unroll=2)

    positions = C * F * R
    long_scale = 1.0 / math.sqrt(positions * width)
    short_scale = 1.0 / math.sqrt(positions)

    def short_grad(t, i):
        grads = d32[i, t, 0:R, :]
        sums = []
        for j in range(SHORT):
            source = pm_ref[i, j - 1, t] if j else x32[i, t, PAD:PAD + R, :]
            sums.append(jnp.sum(grads * source, axis=0, keepdims=True))
        sums.append(jnp.zeros((1, LANES), F32))
        return jnp.concatenate(sums, axis=0) * short_scale

    if remote:
        dz_copy.wait()

    def last_backward(t, carry):
        dzt_ref[t, B] = jnp.transpose(dzh_ref[t])
        backward_rows(t, B - 1)
        for i in (1, 2):
            pay_ref[0, (i - 1) * T + t] = short_grad(t, i)
        return carry

    lax.fori_loop(0, T, last_backward, 0, unroll=2)

    def heads(i):
        return rcopy(d32.at[i, :, pl.ds(0, PAD), :], dh_ref.at[i], HEADS + i, prv)

    def own_slots(owner):
        return pl.ds(owner * per, per)

    def scatter(n):
        return [
            rcopy(
                pay_ref.at[n, own_slots(ctx_peer(d))], rs_ref.at[n, ctx], rs0 + n * C + d,
                {"ctx": ctx_peer(d)},
            )
            for d in range(1, C)
        ]

    sends = []
    if remote:
        for copy in [heads(1), heads(2)] + scatter(0):
            copy.start()
        u_copy.wait()

    sub_all = lax.broadcasted_iota(jnp.int32, (GT * 8, TAPS), 0) & 7

    def last_forward(t, carry):
        ut_ref[t, 0] = jnp.transpose(uh_ref[t])
        forward_rows(t, 0)
        pay_ref[1, t] = short_grad(t, 0)
        return carry

    lax.fori_loop(0, T, last_forward, 0, unroll=2)
    if remote:
        heads(0).start()

    def late_grad(t, carry):
        stack = long_grad(t, B - 1)
        if B > 1:
            stack = stack + gl_ref[t]
        for bit in (1, 2, 4):
            stack = jnp.where((sub_all & bit) != 0, pltpu.roll(stack, LANES - bit, 1), stack)
        pay_ref[1, T + t] = jnp.sum(stack.reshape(GT, 8, TAPS), axis=1) * long_scale
        return carry

    lax.fori_loop(0, T, late_grad, 0, unroll=2)
    if remote:
        for copy in scatter(1):
            copy.start()
        for n in range(2):
            rs_ref[n, ctx] = pay_ref[n, own_slots(ctx)]

    def outputs(i, o_hbm):
        if remote:
            heads(i).wait_recv()
        d32[i, :, R:R + PAD, :] = dh_ref[i]

        def one_block(t, carry):
            total = d32[i, t, pl.ds(0, R), :] * sf_ref[i, 0:1, lane_block(t)]
            for j in range(1, SHORT):
                piece = d32[i, t, pl.ds(j, R), :] * mas_ref[j - 1]
                total = total + piece * sf_ref[i, j:j + 1, lane_block(t)]
            out_ref[i, :, lane_block(t)] = total.astype(BF16)
            return carry

        lax.fori_loop(0, T, one_block, 0)
        store = pltpu.make_async_copy(out_ref.at[i], o_hbm.at[0], osem.at[i])
        store.start()
        return store

    def exchange(n):
        return [
            rcopy(red_ref.at[n, fs], red_ref.at[n, fs], red0 + n * F + d, {"fsdp": fs_peer(d)})
            for d in range(1, F)
        ]

    def gather(n):
        own = fin_ref.at[n, own_slots(ctx)]
        return [rcopy(own, own, ag0 + n * C + d, {"ctx": ctx_peer(d)}) for d in range(1, C)]

    def sum_scattered(n):
        for d in range(1, C):
            sender = lax.rem(ctx + C - d, C)
            rcopy(
                pay_ref.at[n, own_slots(ctx)], rs_ref.at[n, sender], rs0 + n * C + d, {"ctx": ctx_peer(d)}
            ).wait_recv()
        total = rs_ref[n, 0]
        for c in range(1, C):
            total = total + rs_ref[n, c]
        red_ref[n, fs] = total
        for copy in exchange(n):
            copy.start()

    def sum_exchanged(n):
        for d in range(1, F):
            sender = lax.rem(fs + F - d, F)
            rcopy(
                red_ref.at[n, fs], red_ref.at[n, sender], red0 + n * F + d, {"fsdp": fs_peer(d)}
            ).wait_recv()
        total = red_ref[n, 0]
        for f in range(1, F):
            total = total + red_ref[n, f]
        fin_ref[n, own_slots(ctx)] = total
        for copy in gather(n):
            copy.start()

    def wait_gathered(n):
        for d in range(1, C):
            sender = lax.rem(ctx + C - d, C)
            rcopy(
                fin_ref.at[n, own_slots(ctx)], fin_ref.at[n, own_slots(sender)], ag0 + n * C + d,
                {"ctx": ctx_peer(d)},
            ).wait_recv()

    stores = [outputs(1, ok_hbm)]
    if remote:
        sum_scattered(0)
    stores.append(outputs(2, ov_hbm))
    if remote:
        sum_scattered(1)
    stores.append(outputs(0, oq_hbm))
    if remote:
        sum_exchanged(0)
        sum_exchanged(1)
        wait_gathered(0)
        wait_gathered(1)
    for t in range(T):
        lanes = slice(t * LANES, (t + 1) * LANES)
        ogs_ref[0, :, lanes] = fin_ref[1, t, 0:SHORT, :]
        ogs_ref[1, :, lanes] = fin_ref[0, t, 0:SHORT, :]
        ogs_ref[2, :, lanes] = fin_ref[0, T + t, 0:SHORT, :]
    lags = fin_ref[1, T:2 * T].reshape(G, TAPS)
    if G < LANES:
        lags = jnp.concatenate([lags, jnp.zeros((LANES - G, TAPS), F32)], axis=0)
    turn_ref[...] = jnp.transpose(lags)
    ogl_ref[...] = turn_ref[pl.ds(pl.multiple_of(fs * tapw, 8), tapw), :][:, :G]
    for store in stores:
        store.wait()
    if remote:
        for copy in filter_sends + [heads(i) for i in range(3)]:
            copy.wait_send()
        for n in range(2):
            for copy in scatter(n) + exchange(n) + gather(n):
                copy.wait_send()


def mixer(C, F, remote, q_in, k_in, v_in, grad_out, ids, long_filter, short_filter):
    R, channels = q_in.shape[1], q_in.shape[2]
    T, B = channels // LANES, R // TAPS
    G, tapw = long_filter.shape
    per = 2 * T // C
    wide = jax.ShapeDtypeStruct(q_in.shape, BF16)
    copies = FIRST_FREE + 3 * F + 4 * C
    vmem = pltpu.VMEM
    blocks = (T, TAPS, LANES)
    *grads, grad_long, grad_short = pl.pallas_call(
        functools.partial(kernel, (C, F, remote)),
        out_shape=(
            wide, wide, wide,
            jax.ShapeDtypeStruct((tapw, G), F32),
            jax.ShapeDtypeStruct(short_filter.shape, F32),
        ),
        in_specs=[pl.BlockSpec(memory_space=pl.ANY)] * 7,
        out_specs=[pl.BlockSpec(memory_space=pl.ANY)] * 3 + [pl.BlockSpec(memory_space=vmem)] * 2,
        scratch_shapes=[
            vmem((3, R, channels), BF16), vmem((R, channels), BF16),
            vmem((1, R), jnp.int32), vmem((tapw, G), BF16), vmem(short_filter.shape, F32),
            vmem((3, R, channels), BF16),
            vmem((3, T, PAD + R, LANES), F32),
            vmem((3, SHORT - 1, T, R, LANES), F32),
            vmem((T, R, LANES), F32), vmem((T, R, LANES), F32),
            vmem((T, R, LANES), BF16), vmem((T, R, LANES), BF16),
            vmem(blocks, BF16), vmem(blocks, BF16),
            vmem((T, B + 1, LANES, TAPS), BF16), vmem((T, B + 1, LANES, TAPS), BF16),
            vmem((3, TAIL, channels), BF16),
            vmem((1, R), jnp.int32), vmem((1, R), jnp.int32),
            vmem((F, tapw, G), BF16),
            vmem((G, TAPS), F32), vmem((G, TAPS), F32),
            vmem((G, TAPS, TAPS), BF16), vmem((G, TAPS, TAPS), BF16),
            vmem((B, 2, TAPS, LANES), BF16), vmem((B, 2, TAPS, LANES), BF16),
            vmem((B, TAPS, LANES), F32),
            vmem((R + 2 * LANES, LANES), F32),
            vmem((SHORT - 1, R, LANES), F32), vmem((SHORT - 1, R, LANES), F32),
            vmem((3, T, R + PAD, LANES), F32),
            vmem((3, T, PAD, LANES), F32),
            vmem((T, G // T * 8, LANES), F32),
            vmem((TAPS, LANES), F32),
            vmem((2, 2 * T, 8, LANES), F32),
            vmem((2, C, per, 8, LANES), F32),
            vmem((2, F, per, 8, LANES), F32),
            vmem((2, 2 * T, 8, LANES), F32),
            pltpu.SemaphoreType.DMA((copies,)),
            pltpu.SemaphoreType.DMA((copies,)),
            pltpu.SemaphoreType.DMA((7,)),
            pltpu.SemaphoreType.DMA((3,)),
        ],
        compiler_params=pltpu.CompilerParams(
            collective_id=0 if remote else None,
            has_side_effects=True,
            vmem_limit_bytes=60 * 1024 * 1024,
        ),
        name="mixer",
    )(q_in, k_in, v_in, grad_out, ids, long_filter.T, short_filter)
    return (*grads, grad_long.T, grad_short)


def solution(mesh):
    C, F = mesh.shape["ctx"], mesh.shape["fsdp"]
    wide = P("fsdp", "ctx", "tp")
    return jax.shard_map(
        functools.partial(mixer, C, F, True),
        mesh=mesh,
        in_specs=(wide, wide, wide, wide, P("fsdp", "ctx"), P("tp", "fsdp"), P(None, None, "tp")),
        out_specs=(wide, wide, wide, P("tp", "fsdp"), P(None, None, "tp")),
        check_vma=False,
    )
```

time: 88.9 us -> 62.4 us (0.70)
  Pallas kernels: 80.3 us -> 56.3 us
  local copies, waits for them, and re-layouts: 7.57 us -> 5.2 us
    pallas_call x1, Pallas kernels: 80.3 us -> 56.3 us  [mixer(): pl.pallas_call(functools.partial(kernel, (C, F, remote)), out_shape=(wide...]
    pallas_call x1 -> x0, local copies, waits for them, and re-layouts: 1.43 us -> none  [mixer(): pl.pallas_call(functools.partial(kernel, (C, F, remote)), out_shape=(wide...]
    unnamed x11 -> x13, local copies, waits for them, and re-layouts: 6.14 us -> 5.2 us
where the time goes in v1:
time: 62.4 us; the launch traced here: 62.1 us
  Pallas kernels  56.3 us (90%)
  local copies, waits for them, and re-layouts  5.2 us (8%)
  between operations  0.66 us (1%)
    pallas_call x1, Pallas kernels, mixer(): pl.pallas_call(functools.partial(kernel, (C, F, remote)), out_shape=(wide...  56.3 us
    unnamed x13, local copies, waits for them, and re-layouts  5.2 us

profile of v1, /device:TPU:1, one launch (start us, length us, event | category | flops | bytes accessed | tf_op | source)
XLA Modules:
  0.0 62.1 jit_solution(13990693879514441211)
XLA Ops:
  0.6 56.3 %mixer.1 = (bf16[1,256,1024]{2,1,0:T(8,128)(2,1)}, bf16[1,256,1024]{2,1,0:T(8,128)(2,1)}, bf16[1,256,1024]{2,1,0:T(8,128)(2,1)}, f32[16,64]{1,0:T(8,128)}, f32[3,7,1024]{2,1,0:T(8,128)}) custom-call(bf16[1,256,1024]{2,1,0:T(8,128)(2,1)} %q_hbm.1, bf16[1,256,1024]{2,1,0:T(8,128)(2,1)} %k_hbm.1, bf16[1,256,1024]{2,1,0:T(8,128)(2,1)} %v_hbm.1, ...), custom_call_target="tpu_custom_call" | custom-call | tf_op jit(solution)/shard_map/mixer/pallas_call | solution.py:478
  56.9 0.0 copy-start.1
  56.9 1.9 %copy.17 = bf16[1,256,1024]{2,1,0:T(8,128)(2,1)} copy(bf16[1,256,1024]{2,1,0:T(8,128)(2,1)} %get-tuple-element.20) | data formatting | bytes 1048576
  58.9 0.0 copy-done.1
  58.9 0.0 copy-start
  58.9 0.8 %copy.18 = bf16[1,256,1024]{2,1,0:T(8,128)(2,1)} copy(bf16[1,256,1024]{2,1,0:T(8,128)(2,1)S(1)} %copy-done.1) | data formatting | bytes 1048576
  59.7 0.4 copy-done
  60.1 0.0 copy-start.3
  60.1 0.0 copy-start.2
  60.1 0.8 %copy.19 = bf16[1,256,1024]{2,1,0:T(8,128)(2,1)} copy(bf16[1,256,1024]{2,1,0:T(8,128)(2,1)S(1)} %copy-done) | data formatting | bytes 1048576
  60.9 0.0 copy-done.3
  60.9 0.6 copy.20
  61.5 0.0 copy-done.2
  61.5 0.6 %copy.21 = f32[3,7,1024]{2,1,0:T(8,128)} copy(f32[3,7,1024]{2,1,0:T(8,128)S(1)} %copy-done.2) | data formatting | bytes 172032
Async XLA Ops:
  56.9 1.9 %copy-start.1 = (bf16[1,256,1024]{2,1,0:T(8,128)(2,1)S(1)}, bf16[1,256,1024]{2,1,0:T(8,128)(2,1)}, u32[]{:S(2)}) copy-start(bf16[1,256,1024]{2,1,0:T(8,128)(2,1)} %get-tuple-element.21) | copy-start | bytes 1572868
  58.9 1.2 %copy-start = (bf16[1,256,1024]{2,1,0:T(8,128)(2,1)S(1)}, bf16[1,256,1024]{2,1,0:T(8,128)(2,1)}, u32[]{:S(2)}) copy-start(bf16[1,256,1024]{2,1,0:T(8,128)(2,1)} %get-tuple-element.22) | copy-start | bytes 1572868
  60.1 0.8 %copy-start.3 = (f32[16,64]{1,0:T(8,128)S(1)}, f32[16,64]{1,0:T(8,128)}, u32[]{:S(2)}) copy-start(f32[16,64]{1,0:T(8,128)} %get-tuple-element.13) | copy-start | bytes 12292
  60.1 1.4 %copy-start.2 = (f32[3,7,1024]{2,1,0:T(8,128)S(1)}, f32[3,7,1024]{2,1,0:T(8,128)}, u32[]{:S(2)}) copy-start(f32[3,7,1024]{2,1,0:T(8,128)} %get-tuple-element.24) | copy-start | bytes 258052

commit v2 on v1

--- a/solution.py
+++ b/solution.py
@@ -13,13 +13,15 @@
 LANES = 128
 PAD = 8
 TAIL = 16
-CHUNK = 64
+CHUNK = 32
 F32 = jnp.float32
 BF16 = jnp.bfloat16
 MESH = pl.DeviceIdType.MESH
 NT_DIMS = (((1,), (1,)), ((), ()))
 
-TAILS, IDS_DOWN, IDS_UP, U_HALO, DZ_HALO, HEADS, FIRST_FREE = 0, 3, 4, 5, 6, 7, 10
+TAILS, IDS_DOWN, IDS_UP, U_HALO, DZ_HALO, HEADS, FILTERS = 0, 3, 4, 5, 6, 7, 10
+SCATTER, EXCHANGE, GATHER, SLOTS = 11, 14, 17, 20
+STREAMS = 3
 
 
 def kernel(
@@ -30,9 +32,10 @@
     x32, pm_ref, ks_ref, vs_ref, u_ref, dz_ref, uh_ref, dzh_ref, ut_ref, dzt_ref,
     tails_ref, idp_ref, idn_ref,
     lfs_ref, h_ref, hn_ref, ba_ref, bc_ref, mc_ref, ma_ref, mq_ref, idc_ref, ms_ref, mas_ref,
-    d32, dh_ref, gl_ref, turn_ref, pay_ref, rs_ref, red_ref, fin_ref,
-    ssem, rsem, isem, osem,
+    d32, dh_ref, gl_ref, turn_ref, turned_ref, *rest,
 ):
+    pay_refs, rs_refs, red_refs, fin_refs = (rest[n * STREAMS:(n + 1) * STREAMS] for n in range(4))
+    ssem, rsem, isem, osem = rest[4 * STREAMS:]
     C, F, remote = dims
     R = xin_ref.shape[1]
     T = xin_ref.shape[2] // LANES
@@ -45,10 +48,8 @@
     fs = lax.axis_index("fsdp") if remote else 0
     nxt = {"ctx": lax.rem(ctx + 1, C)}
     prv = {"ctx": lax.rem(ctx + C - 1, C)}
-    fil0 = FIRST_FREE
-    rs0 = fil0 + F
-    red0 = rs0 + 2 * C
-    ag0 = red0 + 2 * F
+    ctx_order = sorted(range(1, C), key=lambda d: -min(d, C - d))
+    fs_order = sorted(range(1, F), key=lambda d: (-min(d % (F // 2), F // 2 - d % (F // 2)) - 4 * (d * 2 >= F)))
 
     def rcopy(src, dst, slot, device):
         return pltpu.make_async_remote_copy(
@@ -56,6 +57,9 @@
             device_id=device, device_id_type=MESH,
         )
 
+    def whole(ref, slot):
+        return rcopy(ref, ref, slot, prv)
+
     def ctx_peer(d):
         return lax.rem(ctx + d, C)
 
@@ -64,10 +68,10 @@
 
     if remote:
         barrier = pltpu.get_barrier_semaphore()
-        for d in range(1, C):
+        for d in fs_order:
+            pl.semaphore_signal(barrier, inc=1, device_id={"fsdp": fs_peer(d)}, device_id_type=MESH)
+        for d in ctx_order:
             pl.semaphore_signal(barrier, inc=1, device_id={"ctx": ctx_peer(d)}, device_id_type=MESH)
-        for d in range(1, F):
-            pl.semaphore_signal(barrier, inc=1, device_id={"fsdp": fs_peer(d)}, device_id_type=MESH)
 
     loads = [
         pltpu.make_async_copy(src, dst, isem.at[n])
@@ -138,7 +142,7 @@
     if remote:
         pl.semaphore_wait(barrier, (C - 1) + (F - 1))
         filter_sends = [
-            rcopy(lf_ref, lfs_ref.at[fs], fil0 + d, {"fsdp": fs_peer(d)}) for d in range(1, F)
+            rcopy(lf_ref, lfs_ref.at[fs], FILTERS, {"fsdp": fs_peer(d)}) for d in fs_order
         ]
         tail_copies = [
             rcopy(xin_ref.at[i, pl.ds(R - TAIL, TAIL), :], tails_ref.at[i], TAILS + i, nxt)
@@ -228,7 +232,7 @@
         gl_ref[t] = total
         return carry
 
-    lax.fori_loop(0, T, early_grad, 0, unroll=2)
+    lax.fori_loop(0, T, early_grad, 0, unroll=8)
 
     def turn_own(t, carry):
         for b in range(B):
@@ -236,11 +240,10 @@
             dzt_ref[t, b] = jnp.transpose(dz_ref[t, b * TAPS:(b + 1) * TAPS, :])
         return carry
 
-    lax.fori_loop(0, T, turn_own, 0)
-
-    if remote:
-        for d in range(1, F):
-            rcopy(lf_ref, lfs_ref.at[lax.rem(fs + F - d, F)], fil0 + d, {"fsdp": fs_peer(d)}).wait_recv()
+    lax.fori_loop(0, T, turn_own, 0, unroll=4)
+
+    if remote:
+        whole(lfs_ref.at[pl.ds(0, F - 1)], FILTERS).wait_recv()
     stacked = jnp.concatenate([lfs_ref[s] for s in range(F)], axis=0)
     unit_row = lax.broadcasted_iota(jnp.int32, (G, G), 0)
     unit_col = lax.broadcasted_iota(jnp.int32, (G, G), 1)
@@ -250,7 +253,7 @@
     h_ref[...] = taps
     hn_ref[...] = jnp.dot(taps.astype(BF16), swap, preferred_element_type=F32)
     sub = lax.broadcasted_iota(jnp.int32, (8, TAPS), 0)
-    unroll = 4
+    unroll = 8
 
     def band_of(row):
         base = jnp.broadcast_to(row, (8, TAPS))
@@ -296,7 +299,7 @@
             forward_rows(t, b)
         return carry
 
-    lax.fori_loop(0, T, inner_products, 0, unroll=2)
+    lax.fori_loop(0, T, inner_products, 0, unroll=8)
 
     positions = C * F * R
     long_scale = 1.0 / math.sqrt(positions * width)
@@ -318,10 +321,10 @@
         dzt_ref[t, B] = jnp.transpose(dzh_ref[t])
         backward_rows(t, B - 1)
         for i in (1, 2):
-            pay_ref[0, (i - 1) * T + t] = short_grad(t, i)
-        return carry
-
-    lax.fori_loop(0, T, last_backward, 0, unroll=2)
+            pay_refs[0][(i - 1) * T + t] = short_grad(t, i)
+        return carry
+
+    lax.fori_loop(0, T, last_backward, 0, unroll=8)
 
     def heads(i):
         return rcopy(d32.at[i, :, pl.ds(0, PAD), :], dh_ref.at[i], HEADS + i, prv)
@@ -330,31 +333,23 @@
         return pl.ds(owner * per, per)
 
     def scatter(n):
-        return [
+        for d in ctx_order:
             rcopy(
-                pay_ref.at[n, own_slots(ctx_peer(d))], rs_ref.at[n, ctx], rs0 + n * C + d,
+                pay_refs[n].at[own_slots(ctx_peer(d))], rs_refs[n].at[ctx], SCATTER + n,
                 {"ctx": ctx_peer(d)},
-            )
-            for d in range(1, C)
-        ]
-
-    sends = []
-    if remote:
-        for copy in [heads(1), heads(2)] + scatter(0):
-            copy.start()
-        u_copy.wait()
+            ).start()
+        rs_refs[n][ctx] = pay_refs[n][own_slots(ctx)]
+
+    if remote:
+        scatter(0)
+        heads(1).start()
+        heads(2).start()
 
     sub_all = lax.broadcasted_iota(jnp.int32, (GT * 8, TAPS), 0) & 7
 
-    def last_forward(t, carry):
-        ut_ref[t, 0] = jnp.transpose(uh_ref[t])
-        forward_rows(t, 0)
-        pay_ref[1, t] = short_grad(t, 0)
-        return carry
-
-    lax.fori_loop(0, T, last_forward, 0, unroll=2)
-    if remote:
-        heads(0).start()
+    def put_halves(ref, t, tile):
+        ref[2 * t] = tile[0:4]
+        ref[2 * t + 1] = tile[4:8]
 
     def late_grad(t, carry):
         stack = long_grad(t, B - 1)
@@ -362,15 +357,24 @@
             stack = stack + gl_ref[t]
         for bit in (1, 2, 4):
             stack = jnp.where((sub_all & bit) != 0, pltpu.roll(stack, LANES - bit, 1), stack)
-        pay_ref[1, T + t] = jnp.sum(stack.reshape(GT, 8, TAPS), axis=1) * long_scale
-        return carry
-
-    lax.fori_loop(0, T, late_grad, 0, unroll=2)
-    if remote:
-        for copy in scatter(1):
-            copy.start()
-        for n in range(2):
-            rs_ref[n, ctx] = pay_ref[n, own_slots(ctx)]
+        put_halves(pay_refs[1], t, jnp.sum(stack.reshape(GT, 8, TAPS), axis=1) * long_scale)
+        return carry
+
+    lax.fori_loop(0, T, late_grad, 0, unroll=8)
+    if remote:
+        scatter(1)
+        u_copy.wait()
+
+    def last_forward(t, carry):
+        ut_ref[t, 0] = jnp.transpose(uh_ref[t])
+        forward_rows(t, 0)
+        put_halves(pay_refs[2], t, short_grad(t, 0))
+        return carry
+
+    lax.fori_loop(0, T, last_forward, 0, unroll=8)
+    if remote:
+        scatter(2)
+        heads(0).start()
 
     def outputs(i, o_hbm):
         if remote:
@@ -386,84 +390,96 @@
             return carry
 
         lax.fori_loop(0, T, one_block, 0)
-        store = pltpu.make_async_copy(out_ref.at[i], o_hbm.at[0], osem.at[i])
-        store.start()
-        return store
-
-    def exchange(n):
-        return [
-            rcopy(red_ref.at[n, fs], red_ref.at[n, fs], red0 + n * F + d, {"fsdp": fs_peer(d)})
-            for d in range(1, F)
-        ]
-
-    def gather(n):
-        own = fin_ref.at[n, own_slots(ctx)]
-        return [rcopy(own, own, ag0 + n * C + d, {"ctx": ctx_peer(d)}) for d in range(1, C)]
+        pltpu.make_async_copy(out_ref.at[i], o_hbm.at[0], osem.at[i]).start()
 
     def sum_scattered(n):
-        for d in range(1, C):
-            sender = lax.rem(ctx + C - d, C)
-            rcopy(
-                pay_ref.at[n, own_slots(ctx)], rs_ref.at[n, sender], rs0 + n * C + d, {"ctx": ctx_peer(d)}
-            ).wait_recv()
-        total = rs_ref[n, 0]
+        whole(rs_refs[n].at[pl.ds(0, C - 1)], SCATTER + n).wait_recv()
+        total = rs_refs[n][0]
         for c in range(1, C):
-            total = total + rs_ref[n, c]
-        red_ref[n, fs] = total
-        for copy in exchange(n):
-            copy.start()
+            total = total + rs_refs[n][c]
+        own = red_refs[n].at[fs]
+        own[...] = total
+        for d in fs_order:
+            rcopy(own, own, EXCHANGE + n, {"fsdp": fs_peer(d)}).start()
 
     def sum_exchanged(n):
-        for d in range(1, F):
-            sender = lax.rem(fs + F - d, F)
-            rcopy(
-                red_ref.at[n, fs], red_ref.at[n, sender], red0 + n * F + d, {"fsdp": fs_peer(d)}
-            ).wait_recv()
-        total = red_ref[n, 0]
+        whole(red_refs[n].at[pl.ds(0, F - 1)], EXCHANGE + n).wait_recv()
+        total = red_refs[n][0]
         for f in range(1, F):
-            total = total + red_ref[n, f]
-        fin_ref[n, own_slots(ctx)] = total
-        for copy in gather(n):
-            copy.start()
-
-    def wait_gathered(n):
-        for d in range(1, C):
-            sender = lax.rem(ctx + C - d, C)
-            rcopy(
-                fin_ref.at[n, own_slots(ctx)], fin_ref.at[n, own_slots(sender)], ag0 + n * C + d,
-                {"ctx": ctx_peer(d)},
-            ).wait_recv()
-
-    stores = [outputs(1, ok_hbm)]
+            total = total + red_refs[n][f]
+        own = fin_refs[n].at[own_slots(ctx)]
+        own[...] = total
+        for d in ctx_order:
+            rcopy(own, own, GATHER + n, {"ctx": ctx_peer(d)}).start()
+
+    def others(n):
+        return fin_refs[n].at[pl.ds(0, (C - 1) * per)]
+
+    outputs(1, ok_hbm)
     if remote:
         sum_scattered(0)
-    stores.append(outputs(2, ov_hbm))
+    outputs(2, ov_hbm)
     if remote:
         sum_scattered(1)
-    stores.append(outputs(0, oq_hbm))
-    if remote:
-        sum_exchanged(0)
-        sum_exchanged(1)
-        wait_gathered(0)
-        wait_gathered(1)
+    outputs(0, oq_hbm)
+    if remote:
+        sum_scattered(2)
+        for n in range(STREAMS):
+            sum_exchanged(n)
+        for n in range(STREAMS):
+            whole(others(n), GATHER + n).wait_recv()
     for t in range(T):
         lanes = slice(t * LANES, (t + 1) * LANES)
-        ogs_ref[0, :, lanes] = fin_ref[1, t, 0:SHORT, :]
-        ogs_ref[1, :, lanes] = fin_ref[0, t, 0:SHORT, :]
-        ogs_ref[2, :, lanes] = fin_ref[0, T + t, 0:SHORT, :]
-    lags = fin_ref[1, T:2 * T].reshape(G, TAPS)
+        ogs_ref[0, 0:4, lanes] = fin_refs[2][2 * t]
+        ogs_ref[0, 4:SHORT, lanes] = fin_refs[2][2 * t + 1, 0:SHORT - 4, :]
+        ogs_ref[1, :, lanes] = fin_refs[0][t, 0:SHORT, :]
+        ogs_ref[2, :, lanes] = fin_refs[0][T + t, 0:SHORT, :]
     if G < LANES:
-        lags = jnp.concatenate([lags, jnp.zeros((LANES - G, TAPS), F32)], axis=0)
-    turn_ref[...] = jnp.transpose(lags)
-    ogl_ref[...] = turn_ref[pl.ds(pl.multiple_of(fs * tapw, 8), tapw), :][:, :G]
+        turn_ref[G:, :] = jnp.zeros((LANES - G, TAPS), F32)
+    for n in range(2 * T):
+        turn_ref[4 * n:4 * n + 4, :] = fin_refs[1][n]
+    turned_ref[...] = jnp.transpose(turn_ref[...])
+    ogl_ref[...] = turned_ref[pl.ds(pl.multiple_of(fs * tapw, 8), tapw), :][:, :G]
+    for i, o_hbm in enumerate((oq_hbm, ok_hbm, ov_hbm)):
+        pltpu.make_async_copy(out_ref.at[i], o_hbm.at[0], osem.at[i]).wait()
+    if remote:
+        whole(lfs_ref.at[pl.ds(0, F - 1)], FILTERS).wait_send()
+        for i in range(3):
+            heads(i).wait_send()
+        for n in range(STREAMS):
+            whole(rs_refs[n].at[pl.ds(0, C - 1)], SCATTER + n).wait_send()
+            whole(red_refs[n].at[pl.ds(0, F - 1)], EXCHANGE + n).wait_send()
+            whole(others(n), GATHER + n).wait_send()
+
+
+def settle(*refs):
+    count = (len(refs) - 2) // 3
+    sources, targets, held = refs[:count], refs[count:2 * count], refs[2 * count:3 * count]
+    in_sem, out_sem = refs[3 * count:]
+    loads = [pltpu.make_async_copy(a, b, in_sem.at[n]) for n, (a, b) in enumerate(zip(sources, held))]
+    stores = [pltpu.make_async_copy(a, b, out_sem.at[n]) for n, (a, b) in enumerate(zip(held, targets))]
+    for load in loads:
+        load.start()
+    for load, store in zip(loads, stores):
+        load.wait()
+        store.start()
     for store in stores:
         store.wait()
-    if remote:
-        for copy in filter_sends + [heads(i) for i in range(3)]:
-            copy.wait_send()
-        for n in range(2):
-            for copy in scatter(n) + exchange(n) + gather(n):
-                copy.wait_send()
+
+
+def settled(arrays):
+    anywhere = [pl.BlockSpec(memory_space=pl.ANY)] * len(arrays)
+    shapes = [jax.ShapeDtypeStruct(a.shape, a.dtype) for a in arrays]
+    return pl.pallas_call(
+        settle,
+        out_shape=shapes,
+        in_specs=anywhere,
+        out_specs=anywhere,
+        scratch_shapes=[pltpu.VMEM(a.shape, a.dtype) for a in arrays]
+        + [pltpu.SemaphoreType.DMA((len(arrays),))] * 2,
+        compiler_params=pltpu.CompilerParams(vmem_limit_bytes=60 * 1024 * 1024),
+        name="settle",
+    )(*arrays)
 
 
 def mixer(C, F, remote, q_in, k_in, v_in, grad_out, ids, long_filter, short_filter):
@@ -472,10 +488,10 @@
     G, tapw = long_filter.shape
     per = 2 * T // C
     wide = jax.ShapeDtypeStruct(q_in.shape, BF16)
-    copies = FIRST_FREE + 3 * F + 4 * C
+    heights = (8, 4, 4)
     vmem = pltpu.VMEM
     blocks = (T, TAPS, LANES)
-    *grads, grad_long, grad_short = pl.pallas_call(
+    results = pl.pallas_call(
         functools.partial(kernel, (C, F, remote)),
         out_shape=(
             wide, wide, wide,
@@ -506,13 +522,13 @@
             vmem((3, T, R + PAD, LANES), F32),
             vmem((3, T, PAD, LANES), F32),
             vmem((T, G // T * 8, LANES), F32),
-            vmem((TAPS, LANES), F32),
-            vmem((2, 2 * T, 8, LANES), F32),
-            vmem((2, C, per, 8, LANES), F32),
-            vmem((2, F, per, 8, LANES), F32),
-            vmem((2, 2 * T, 8, LANES), F32),
-            pltpu.SemaphoreType.DMA((copies,)),
-            pltpu.SemaphoreType.DMA((copies,)),
+            vmem((TAPS, LANES), F32), vmem((TAPS, LANES), F32),
+            *(vmem((2 * T, h, LANES), F32) for h in heights),
+            *(vmem((C, per, h, LANES), F32) for h in heights),
+            *(vmem((F, per, h, LANES), F32) for h in heights),
+            *(vmem((2 * T, h, LANES), F32) for h in heights),
+            pltpu.SemaphoreType.DMA((SLOTS,)),
+            pltpu.SemaphoreType.DMA((SLOTS,)),
             pltpu.SemaphoreType.DMA((7,)),
             pltpu.SemaphoreType.DMA((3,)),
         ],
@@ -523,6 +539,7 @@
         ),
         name="mixer",
     )(q_in, k_in, v_in, grad_out, ids, long_filter.T, short_filter)
+    *grads, grad_long, grad_short = settled(results)
     return (*grads, grad_long.T, grad_short)
 
 

time: 62.4 us -> 52.2 us (0.84)
  local copies, waits for them, and re-layouts: 5.2 us -> 0 us
  Pallas kernels: 56.3 us -> 51.4 us
    pallas_call x1, Pallas kernels: 56.3 us -> 49.1 us  [mixer(): pl.pallas_call(functools.partial(kernel, (C, F, remote)), out_shape=(wide...]
    unnamed x13 -> x0, local copies, waits for them, and re-layouts: 5.2 us -> none
    pallas_call x0 -> x1, Pallas kernels: none -> 2.29 us  [settled(): pl.pallas_call(settle, out_shape=shapes, in_specs=anywhere, out_specs=any...]
where the time goes in v2:
time: 52.2 us; the launch traced here: 52 us
  Pallas kernels  51.4 us (98%)
  between operations  0.64 us (1%)
    pallas_call x1, Pallas kernels, mixer(): pl.pallas_call(functools.partial(kernel, (C, F, remote)), out_shape=(wide...  49.1 us
    pallas_call x1, Pallas kernels, settled(): pl.pallas_call(settle, out_shape=shapes, in_specs=anywhere, out_specs=any...  2.29 us

profile of v2, /device:TPU:1, one launch (start us, length us, event | category | flops | bytes accessed | tf_op | source)
XLA Modules:
  0.0 52.0 jit_solution(15216102045618687441)
XLA Ops:
  0.6 49.1 %mixer.1 = (bf16[1,256,1024]{2,1,0:T(8,128)(2,1)}, bf16[1,256,1024]{2,1,0:T(8,128)(2,1)}, bf16[1,256,1024]{2,1,0:T(8,128)(2,1)}, f32[16,64]{1,0:T(8,128)}, f32[3,7,1024]{2,1,0:T(8,128)}) custom-call(bf16[1,256,1024]{2,1,0:T(8,128)(2,1)} %q_hbm.1, bf16[1,256,1024]{2,1,0:T(8,128)(2,1)} %k_hbm.1, bf16[1,256,1024]{2,1,0:T(8,128)(2,1)} %v_hbm.1, ...), custom_call_target="tpu_custom_call" | custom-call | tf_op jit(solution)/shard_map/mixer/pallas_call | solution.py:494
  49.7 2.3 %settle.1 = (bf16[1,256,1024]{2,1,0:T(8,128)(2,1)}, bf16[1,256,1024]{2,1,0:T(8,128)(2,1)}, bf16[1,256,1024]{2,1,0:T(8,128)(2,1)}, f32[16,64]{1,0:T(8,128)}, f32[3,7,1024]{2,1,0:T(8,128)}) custom-call(bf16[1,256,1024]{2,1,0:T(8,128)(2,1)} %get-tuple-element.15.refs_0_, bf16[1,256,1024]{2,1,0:T(8,128)(2,1)} %get-tuple-element.16.refs_1_, ...), custom_call_target="tpu_custom_call" | custom-call | tf_op jit(solution)/shard_map/settle/pallas_call | solution.py:473

commit v3 on v2

--- a/solution.py
+++ b/solution.py
@@ -22,6 +22,7 @@
 TAILS, IDS_DOWN, IDS_UP, U_HALO, DZ_HALO, HEADS, FILTERS = 0, 3, 4, 5, 6, 7, 10
 SCATTER, EXCHANGE, GATHER, SLOTS = 11, 14, 17, 20
 STREAMS = 3
+CORES = 2
 
 
 def kernel(
@@ -43,13 +44,21 @@
     tapw, G = lf_ref.shape
     GT = G // T
     width = LANES // GT
-    per = 2 * T // C
+    pers = [tiles // (min(4, F) * CORES) for tiles in (2 * T, T, T)]
     ctx = lax.axis_index("ctx") if remote else 0
     fs = lax.axis_index("fsdp") if remote else 0
     nxt = {"ctx": lax.rem(ctx + 1, C)}
     prv = {"ctx": lax.rem(ctx + C - 1, C)}
-    ctx_order = sorted(range(1, C), key=lambda d: -min(d, C - d))
-    fs_order = sorted(range(1, F), key=lambda d: (-min(d % (F // 2), F // 2 - d % (F // 2)) - 4 * (d * 2 >= F)))
+    XS = min(4, F)
+    ZS, YS = F // XS, C // CORES
+    z, x, y, core = fs // XS, fs % XS, ctx // CORES, ctx % CORES
+    near_count, far_count = XS * CORES, ZS * YS
+    near, far = x * CORES + core, z * YS + y
+    ring = lambda d, n: min(d, n - d)
+    fs_order = sorted(range(1, F), key=lambda d: -ring(d % XS, XS) - 4 * (d >= XS))
+    near_order = sorted(range(1, near_count), key=lambda d: -ring(d, near_count))
+    far_order = [(dz, dy) for dz in range(ZS) for dy in range(YS) if dz or dy]
+    far_order.sort(key=lambda p: -ring(p[1], YS) - 4 * p[0])
 
     def rcopy(src, dst, slot, device):
         return pltpu.make_async_remote_copy(
@@ -60,8 +69,12 @@
     def whole(ref, slot):
         return rcopy(ref, ref, slot, prv)
 
-    def ctx_peer(d):
-        return lax.rem(ctx + d, C)
+    def near_peer(d):
+        index = (near + d) % near_count
+        return index, {"fsdp": z * XS + index // CORES, "ctx": y * CORES + index % CORES}
+
+    def far_peer(dz, dy):
+        return {"fsdp": (z + dz) % ZS * XS + x, "ctx": (y + dy) % YS * CORES + core}
 
     def fs_peer(d):
         return lax.rem(fs + d, F)
@@ -70,8 +83,13 @@
         barrier = pltpu.get_barrier_semaphore()
         for d in fs_order:
             pl.semaphore_signal(barrier, inc=1, device_id={"fsdp": fs_peer(d)}, device_id_type=MESH)
-        for d in ctx_order:
-            pl.semaphore_signal(barrier, inc=1, device_id={"ctx": ctx_peer(d)}, device_id_type=MESH)
+        greeted = [far_peer(dz, dy) for dz, dy in far_order if dy]
+        greeted += [
+            {"fsdp": z * XS + (x + dx) % XS, "ctx": y * CORES + 1 - core} for dx in range(XS)
+        ]
+        greeted.append({"ctx": (ctx + 2 * core - 1 + C) % C})
+        for device in greeted:
+            pl.semaphore_signal(barrier, inc=1, device_id=device, device_id_type=MESH)
 
     loads = [
         pltpu.make_async_copy(src, dst, isem.at[n])
@@ -140,7 +158,7 @@
 
     loads[6].wait()
     if remote:
-        pl.semaphore_wait(barrier, (C - 1) + (F - 1))
+        pl.semaphore_wait(barrier, len(greeted) + F - 1)
         filter_sends = [
             rcopy(lf_ref, lfs_ref.at[fs], FILTERS, {"fsdp": fs_peer(d)}) for d in fs_order
         ]
@@ -195,10 +213,10 @@
     for b in range(B):
         column = idc_ref[(1 + b) * LANES:(2 + b) * LANES, :]
         same = [jnp.where(column == rows[b + n], one, zero) for n in range(3)]
-        mc_ref[b, 0] = (same[0] * above).astype(BF16)
-        mc_ref[b, 1] = (same[1] * (one - above)).astype(BF16)
-        ma_ref[b, 0] = (same[1] * upper).astype(BF16)
-        ma_ref[b, 1] = (same[2] * (one - upper)).astype(BF16)
+        mc_ref[b, :, :LANES] = (same[0] * above).astype(BF16)
+        mc_ref[b, :, LANES:] = (same[1] * (one - above)).astype(BF16)
+        ma_ref[b, :, :LANES] = (same[1] * upper).astype(BF16)
+        ma_ref[b, :, LANES:] = (same[2] * (one - upper)).astype(BF16)
         mq_ref[b] = same[1] * upper + same[2] * (one - upper)
 
     def dz_window(t, b):
@@ -215,21 +233,16 @@
         left = jnp.concatenate([signal * group_lanes[g] for g in range(GT)], axis=0)
         product = lax.dot_general(left, dz_window(t, b), NT_DIMS, preferred_element_type=F32)
         mask = mq_ref[b]
-        folded = []
+        parts = []
         for g in range(GT):
             part = product[g * TAPS:(g + 1) * TAPS]
-            part = jnp.where(in_upper, part[:, :LANES], part[:, LANES:]) * mask
-            total = part[0:8]
-            for a in range(1, TAPS // 8):
-                total = total + pltpu.roll(part[8 * a:8 * a + 8], LANES - 8 * a, 1)
-            folded.append(total)
-        return jnp.concatenate(folded, axis=0)
+            parts.append(jnp.where(in_upper, part[:, :LANES], part[:, LANES:]) * mask)
+        return parts
 
     def early_grad(t, carry):
-        total = long_grad(t, 0)
-        for b in range(1, B - 1):
-            total = total + long_grad(t, b)
-        gl_ref[t] = total
+        for b in range(B - 1):
+            for g, part in enumerate(long_grad(t, b)):
+                gl_ref[t * GT + g] = part if b == 0 else gl_ref[t * GT + g] + part
         return carry
 
     lax.fori_loop(0, T, early_grad, 0, unroll=8)
@@ -265,8 +278,9 @@
     def build(n, carry):
         for m in range(unroll):
             g = n * unroll + m
-            ba_ref[g] = band_of(h_ref[pl.ds(g, 1), :])
-            bc_ref[g] = band_of(hn_ref[pl.ds(g, 1), :])
+            for band_ref, row_ref in ((ba_ref, h_ref), (bc_ref, hn_ref)):
+                band = band_of(row_ref[pl.ds(g, 1), :])
+                band_ref[g] = jnp.concatenate([band, band], axis=1)
         return carry
 
     lax.fori_loop(0, G // unroll, build, 0)
@@ -275,7 +289,7 @@
         parts = []
         for g in range(GT):
             band = band_ref[t * GT + g]
-            weights = jnp.concatenate([band * mask_ref[b, 0], band * mask_ref[b, 1]], axis=1)
+            weights = band * mask_ref[b]
             rows_g = slice(g * width, (g + 1) * width)
             left = jnp.concatenate([left_ref[t, first, rows_g, :], left_ref[t, first + 1, rows_g, :]], axis=1)
             parts.append(lax.dot_general(left, weights, NT_DIMS, preferred_element_type=F32))
@@ -329,16 +343,14 @@
     def heads(i):
         return rcopy(d32.at[i, :, pl.ds(0, PAD), :], dh_ref.at[i], HEADS + i, prv)
 
-    def own_slots(owner):
-        return pl.ds(owner * per, per)
+    def own_slots(n, owner):
+        return pl.ds(owner * pers[n], pers[n])
 
     def scatter(n):
-        for d in ctx_order:
-            rcopy(
-                pay_refs[n].at[own_slots(ctx_peer(d))], rs_refs[n].at[ctx], SCATTER + n,
-                {"ctx": ctx_peer(d)},
-            ).start()
-        rs_refs[n][ctx] = pay_refs[n][own_slots(ctx)]
+        for d in near_order:
+            index, device = near_peer(d)
+            rcopy(pay_refs[n].at[own_slots(n, index)], rs_refs[n].at[near], SCATTER + n, device).start()
+        rs_refs[n][near] = pay_refs[n][own_slots(n, near)]
 
     if remote:
         scatter(0)
@@ -347,17 +359,19 @@
 
     sub_all = lax.broadcasted_iota(jnp.int32, (GT * 8, TAPS), 0) & 7
 
-    def put_halves(ref, t, tile):
-        ref[2 * t] = tile[0:4]
-        ref[2 * t + 1] = tile[4:8]
-
     def late_grad(t, carry):
-        stack = long_grad(t, B - 1)
-        if B > 1:
-            stack = stack + gl_ref[t]
+        folded = []
+        for g, part in enumerate(long_grad(t, B - 1)):
+            if B > 1:
+                part = part + gl_ref[t * GT + g]
+            total = part[0:8]
+            for a in range(1, TAPS // 8):
+                total = total + pltpu.roll(part[8 * a:8 * a + 8], LANES - 8 * a, 1)
+            folded.append(total)
+        stack = jnp.concatenate(folded, axis=0)
         for bit in (1, 2, 4):
             stack = jnp.where((sub_all & bit) != 0, pltpu.roll(stack, LANES - bit, 1), stack)
-        put_halves(pay_refs[1], t, jnp.sum(stack.reshape(GT, 8, TAPS), axis=1) * long_scale)
+        pay_refs[1][t] = jnp.sum(stack.reshape(GT, 8, TAPS), axis=1) * long_scale
         return carry
 
     lax.fori_loop(0, T, late_grad, 0, unroll=8)
@@ -368,7 +382,7 @@
     def last_forward(t, carry):
         ut_ref[t, 0] = jnp.transpose(uh_ref[t])
         forward_rows(t, 0)
-        put_halves(pay_refs[2], t, short_grad(t, 0))
+        pay_refs[2][t] = short_grad(t, 0)
         return carry
 
     lax.fori_loop(0, T, last_forward, 0, unroll=8)
@@ -393,27 +407,27 @@
         pltpu.make_async_copy(out_ref.at[i], o_hbm.at[0], osem.at[i]).start()
 
     def sum_scattered(n):
-        whole(rs_refs[n].at[pl.ds(0, C - 1)], SCATTER + n).wait_recv()
+        whole(rs_refs[n].at[pl.ds(0, near_count - 1)], SCATTER + n).wait_recv()
         total = rs_refs[n][0]
-        for c in range(1, C):
+        for c in range(1, near_count):
             total = total + rs_refs[n][c]
-        own = red_refs[n].at[fs]
+        own = red_refs[n].at[far]
         own[...] = total
-        for d in fs_order:
-            rcopy(own, own, EXCHANGE + n, {"fsdp": fs_peer(d)}).start()
+        for dz, dy in far_order:
+            rcopy(own, own, EXCHANGE + n, far_peer(dz, dy)).start()
 
     def sum_exchanged(n):
-        whole(red_refs[n].at[pl.ds(0, F - 1)], EXCHANGE + n).wait_recv()
+        whole(red_refs[n].at[pl.ds(0, far_count - 1)], EXCHANGE + n).wait_recv()
         total = red_refs[n][0]
-        for f in range(1, F):
+        for f in range(1, far_count):
             total = total + red_refs[n][f]
-        own = fin_refs[n].at[own_slots(ctx)]
+        own = fin_refs[n].at[own_slots(n, near)]
         own[...] = total
-        for d in ctx_order:
-            rcopy(own, own, GATHER + n, {"ctx": ctx_peer(d)}).start()
+        for d in near_order:
+            rcopy(own, own, GATHER + n, near_peer(d)[1]).start()
 
     def others(n):
-        return fin_refs[n].at[pl.ds(0, (C - 1) * per)]
+        return fin_refs[n].at[pl.ds(0, (near_count - 1) * pers[n])]
 
     outputs(1, ok_hbm)
     if remote:
@@ -430,14 +444,13 @@
             whole(others(n), GATHER + n).wait_recv()
     for t in range(T):
         lanes = slice(t * LANES, (t + 1) * LANES)
-        ogs_ref[0, 0:4, lanes] = fin_refs[2][2 * t]
-        ogs_ref[0, 4:SHORT, lanes] = fin_refs[2][2 * t + 1, 0:SHORT - 4, :]
+        ogs_ref[0, :, lanes] = fin_refs[2][t, 0:SHORT, :]
         ogs_ref[1, :, lanes] = fin_refs[0][t, 0:SHORT, :]
         ogs_ref[2, :, lanes] = fin_refs[0][T + t, 0:SHORT, :]
     if G < LANES:
         turn_ref[G:, :] = jnp.zeros((LANES - G, TAPS), F32)
-    for n in range(2 * T):
-        turn_ref[4 * n:4 * n + 4, :] = fin_refs[1][n]
+    for t in range(T):
+        turn_ref[GT * t:GT * t + GT, :] = fin_refs[1][t]
     turned_ref[...] = jnp.transpose(turn_ref[...])
     ogl_ref[...] = turned_ref[pl.ds(pl.multiple_of(fs * tapw, 8), tapw), :][:, :G]
     for i, o_hbm in enumerate((oq_hbm, ok_hbm, ov_hbm)):
@@ -447,8 +460,8 @@
         for i in range(3):
             heads(i).wait_send()
         for n in range(STREAMS):
-            whole(rs_refs[n].at[pl.ds(0, C - 1)], SCATTER + n).wait_send()
-            whole(red_refs[n].at[pl.ds(0, F - 1)], EXCHANGE + n).wait_send()
+            whole(rs_refs[n].at[pl.ds(0, near_count - 1)], SCATTER + n).wait_send()
+            whole(red_refs[n].at[pl.ds(0, far_count - 1)], EXCHANGE + n).wait_send()
             whole(others(n), GATHER + n).wait_send()
 
 
@@ -486,9 +499,10 @@
     R, channels = q_in.shape[1], q_in.shape[2]
     T, B = channels // LANES, R // TAPS
     G, tapw = long_filter.shape
-    per = 2 * T // C
     wide = jax.ShapeDtypeStruct(q_in.shape, BF16)
-    heights = (8, 4, 4)
+    streams = (2 * T, T, T)
+    near = min(4, F) * CORES
+    far = C * F // near
     vmem = pltpu.VMEM
     blocks = (T, TAPS, LANES)
     results = pl.pallas_call(
@@ -514,19 +528,19 @@
             vmem((1, R), jnp.int32), vmem((1, R), jnp.int32),
             vmem((F, tapw, G), BF16),
             vmem((G, TAPS), F32), vmem((G, TAPS), F32),
-            vmem((G, TAPS, TAPS), BF16), vmem((G, TAPS, TAPS), BF16),
-            vmem((B, 2, TAPS, LANES), BF16), vmem((B, 2, TAPS, LANES), BF16),
+            vmem((G, TAPS, 2 * TAPS), BF16), vmem((G, TAPS, 2 * TAPS), BF16),
+            vmem((B, TAPS, 2 * LANES), BF16), vmem((B, TAPS, 2 * LANES), BF16),
             vmem((B, TAPS, LANES), F32),
             vmem((R + 2 * LANES, LANES), F32),
             vmem((SHORT - 1, R, LANES), F32), vmem((SHORT - 1, R, LANES), F32),
             vmem((3, T, R + PAD, LANES), F32),
             vmem((3, T, PAD, LANES), F32),
-            vmem((T, G // T * 8, LANES), F32),
+            vmem((G, TAPS, LANES), F32),
             vmem((TAPS, LANES), F32), vmem((TAPS, LANES), F32),
-            *(vmem((2 * T, h, LANES), F32) for h in heights),
-            *(vmem((C, per, h, LANES), F32) for h in heights),
-            *(vmem((F, per, h, LANES), F32) for h in heights),
-            *(vmem((2 * T, h, LANES), F32) for h in heights),
+            *(vmem((tiles, 8, LANES), F32) for tiles in streams),
+            *(vmem((near, tiles // near, 8, LANES), F32) for tiles in streams),
+            *(vmem((far, tiles // near, 8, LANES), F32) for tiles in streams),
+            *(vmem((tiles, 8, LANES), F32) for tiles in streams),
             pltpu.SemaphoreType.DMA((SLOTS,)),
             pltpu.SemaphoreType.DMA((SLOTS,)),
             pltpu.SemaphoreType.DMA((7,)),

time: 52.2 us -> 52.5 us (level)
  no operation moved by 1% of the time
where the time goes in v3:
time: 52.5 us; the launch traced here: 52.4 us
  Pallas kernels  51.7 us (98%)
  between operations  0.64 us (1%)
    pallas_call x1, Pallas kernels, mixer(): pl.pallas_call(functools.partial(kernel, (C, F, remote)), out_shape=(wide...  49.4 us
    pallas_call x1, Pallas kernels, settled(): pl.pallas_call(settle, out_shape=shapes, in_specs=anywhere, out_specs=any...  2.29 us

profile of v3, /device:TPU:1, one launch (start us, length us, event | category | flops | bytes accessed | tf_op | source)
XLA Modules:
  0.0 52.4 jit_solution(11903392060950841338)
XLA Ops:
  0.6 49.4 %mixer.1 = (bf16[1,256,1024]{2,1,0:T(8,128)(2,1)}, bf16[1,256,1024]{2,1,0:T(8,128)(2,1)}, bf16[1,256,1024]{2,1,0:T(8,128)(2,1)}, f32[16,64]{1,0:T(8,128)}, f32[3,7,1024]{2,1,0:T(8,128)}) custom-call(bf16[1,256,1024]{2,1,0:T(8,128)(2,1)} %q_hbm.1, bf16[1,256,1024]{2,1,0:T(8,128)(2,1)} %k_hbm.1, bf16[1,256,1024]{2,1,0:T(8,128)(2,1)} %v_hbm.1, ...), custom_call_target="tpu_custom_call" | custom-call | tf_op jit(solution)/shard_map/mixer/pallas_call | solution.py:508
  50.1 2.3 %settle.1 = (bf16[1,256,1024]{2,1,0:T(8,128)(2,1)}, bf16[1,256,1024]{2,1,0:T(8,128)(2,1)}, bf16[1,256,1024]{2,1,0:T(8,128)(2,1)}, f32[16,64]{1,0:T(8,128)}, f32[3,7,1024]{2,1,0:T(8,128)}) custom-call(bf16[1,256,1024]{2,1,0:T(8,128)(2,1)} %get-tuple-element.15.refs_0_, bf16[1,256,1024]{2,1,0:T(8,128)(2,1)} %get-tuple-element.16.refs_1_, ...), custom_call_target="tpu_custom_call" | custom-call | tf_op jit(solution)/shard_map/settle/pallas_call | solution.py:486

commit v4 on v3

--- a/solution.py
+++ b/solution.py
@@ -91,12 +91,20 @@
         for device in greeted:
             pl.semaphore_signal(barrier, inc=1, device_id=device, device_id_type=MESH)
 
+    early = (T + 1) // 2
+    half = early * LANES
+    wide_loads = [
+        (src.at[0, :, lanes], dst.at[:, lanes])
+        for lanes in (pl.ds(0, half), pl.ds(half, T * LANES - half))
+        for src, dst in (
+            (q_hbm, xin_ref.at[0]), (k_hbm, xin_ref.at[1]), (v_hbm, xin_ref.at[2]), (g_hbm, g_ref),
+        )
+    ]
     loads = [
         pltpu.make_async_copy(src, dst, isem.at[n])
-        for n, (src, dst) in enumerate((
-            (ids_hbm, ids_ref), (q_hbm.at[0], xin_ref.at[0]), (k_hbm.at[0], xin_ref.at[1]),
-            (v_hbm.at[0], xin_ref.at[2]), (sf_hbm, sf_ref), (g_hbm.at[0], g_ref), (lf_hbm, lf_ref),
-        ))
+        for n, (src, dst) in enumerate(
+            [(ids_hbm, ids_ref), (sf_hbm, sf_ref)] + wide_loads + [(lf_hbm, lf_ref)]
+        )
     ]
     for load in loads:
         load.start()
@@ -153,10 +161,10 @@
             short_rows(t, r0, CHUNK)
         return carry
 
-    early = (T + 1) // 2
     lax.fori_loop(0, early, short_main, 0)
 
-    loads[6].wait()
+    for load in loads[6:]:
+        load.wait()
     if remote:
         pl.semaphore_wait(barrier, len(greeted) + F - 1)
         filter_sends = [
@@ -352,6 +360,16 @@
             rcopy(pay_refs[n].at[own_slots(n, index)], rs_refs[n].at[near], SCATTER + n, device).start()
         rs_refs[n][near] = pay_refs[n][own_slots(n, near)]
 
+    def sum_scattered(n):
+        whole(rs_refs[n].at[pl.ds(0, near_count - 1)], SCATTER + n).wait_recv()
+        total = rs_refs[n][0]
+        for c in range(1, near_count):
+            total = total + rs_refs[n][c]
+        own = red_refs[n].at[far]
+        own[...] = total
+        for dz, dy in far_order:
+            rcopy(own, own, EXCHANGE + n, far_peer(dz, dy)).start()
+
     if remote:
         scatter(0)
         heads(1).start()
@@ -377,6 +395,7 @@
     lax.fori_loop(0, T, late_grad, 0, unroll=8)
     if remote:
         scatter(1)
+        sum_scattered(0)
         u_copy.wait()
 
     def last_forward(t, carry):
@@ -389,6 +408,7 @@
     if remote:
         scatter(2)
         heads(0).start()
+        sum_scattered(1)
 
     def outputs(i, o_hbm):
         if remote:
@@ -405,16 +425,6 @@
 
         lax.fori_loop(0, T, one_block, 0)
         pltpu.make_async_copy(out_ref.at[i], o_hbm.at[0], osem.at[i]).start()
-
-    def sum_scattered(n):
-        whole(rs_refs[n].at[pl.ds(0, near_count - 1)], SCATTER + n).wait_recv()
-        total = rs_refs[n][0]
-        for c in range(1, near_count):
-            total = total + rs_refs[n][c]
-        own = red_refs[n].at[far]
-        own[...] = total
-        for dz, dy in far_order:
-            rcopy(own, own, EXCHANGE + n, far_peer(dz, dy)).start()
 
     def sum_exchanged(n):
         whole(red_refs[n].at[pl.ds(0, far_count - 1)], EXCHANGE + n).wait_recv()
@@ -431,15 +441,14 @@
 
     outputs(1, ok_hbm)
     if remote:
-        sum_scattered(0)
+        sum_scattered(2)
     outputs(2, ov_hbm)
     if remote:
-        sum_scattered(1)
+        sum_exchanged(0)
     outputs(0, oq_hbm)
     if remote:
-        sum_scattered(2)
-        for n in range(STREAMS):
-            sum_exchanged(n)
+        sum_exchanged(1)
+        sum_exchanged(2)
         for n in range(STREAMS):
             whole(others(n), GATHER + n).wait_recv()
     for t in range(T):
@@ -543,7 +552,7 @@
             *(vmem((tiles, 8, LANES), F32) for tiles in streams),
             pltpu.SemaphoreType.DMA((SLOTS,)),
             pltpu.SemaphoreType.DMA((SLOTS,)),
-            pltpu.SemaphoreType.DMA((7,)),
+            pltpu.SemaphoreType.DMA((11,)),
             pltpu.SemaphoreType.DMA((3,)),
         ],
         compiler_params=pltpu.CompilerParams(

time: 52.5 us -> 53.4 us (1.017)
  Pallas kernels: 51.7 us -> 52.5 us
    pallas_call x1, Pallas kernels: 49.4 us -> 50.3 us  [mixer(): pl.pallas_call(functools.partial(kernel, (C, F, remote)), out_shape=(wide...]
where the time goes in v4:
time: 53.4 us; the launch traced here: 53.2 us
  Pallas kernels  52.5 us (98%)
  between operations  0.64 us (1%)
    pallas_call x1, Pallas kernels, mixer(): pl.pallas_call(functools.partial(kernel, (C, F, remote)), out_shape=(wide...  50.3 us
    pallas_call x1, Pallas kernels, settled(): pl.pallas_call(settle, out_shape=shapes, in_specs=anywhere, out_specs=any...  2.29 us

profile of v4, /device:TPU:1, one launch (start us, length us, event | category | flops | bytes accessed | tf_op | source)
XLA Modules:
  0.0 53.2 jit_solution(8281181090249763882)
XLA Ops:
  0.6 50.3 %mixer.1 = (bf16[1,256,1024]{2,1,0:T(8,128)(2,1)}, bf16[1,256,1024]{2,1,0:T(8,128)(2,1)}, bf16[1,256,1024]{2,1,0:T(8,128)(2,1)}, f32[16,64]{1,0:T(8,128)}, f32[3,7,1024]{2,1,0:T(8,128)}) custom-call(bf16[1,256,1024]{2,1,0:T(8,128)(2,1)} %q_hbm.1, bf16[1,256,1024]{2,1,0:T(8,128)(2,1)} %k_hbm.1, bf16[1,256,1024]{2,1,0:T(8,128)(2,1)} %v_hbm.1, ...), custom_call_target="tpu_custom_call" | custom-call | tf_op jit(solution)/shard_map/mixer/pallas_call | solution.py:517
  50.9 2.3 %settle.1 = (bf16[1,256,1024]{2,1,0:T(8,128)(2,1)}, bf16[1,256,1024]{2,1,0:T(8,128)(2,1)}, bf16[1,256,1024]{2,1,0:T(8,128)(2,1)}, f32[16,64]{1,0:T(8,128)}, f32[3,7,1024]{2,1,0:T(8,128)}) custom-call(bf16[1,256,1024]{2,1,0:T(8,128)(2,1)} %get-tuple-element.15.refs_0_, bf16[1,256,1024]{2,1,0:T(8,128)(2,1)} %get-tuple-element.16.refs_1_, ...), custom_call_target="tpu_custom_call" | custom-call | tf_op jit(solution)/shard_map/settle/pallas_call | solution.py:495
